TPU v7x, 256 devices: a whole 4x4x8 slice. The times are simulated.
256 devices in a mesh: space: 64 (over x, z, core), slide: 4 (over y).
Axes of the slice: x: 4, y: 4, z: 8, core: 2. Of those that a mesh axis runs over, the one named last changes fastest.
Arguments:
- image: bfloat16 [4, 96, 1024, 128], P('slide', None, 'space'), may hold values from -6 to 6
- cotangent: bfloat16 [4, 96, 1024, 128], P('slide', None, 'space'), may hold values from -6 to 6
- tissue: int32 [4, 64, 8], P('slide', 'space'), may hold values from 0 to 1, as said below
- dw_kernel: float32 [96, 49], replicated, may hold values from -0.875 to 0.875
- dw_bias: float32 [96], replicated, may hold values from -3 to 3
- ln_gain: float32 [96], replicated, may hold values from 0.5 to 1.5
- ln_bias: float32 [96], replicated, may hold values from -2 to 2
- w_in: bfloat16 [96, 384], replicated, may hold values from -0.625 to 0.625
- b_in: float32 [384], replicated, may hold values from -3 to 3
- w_out: bfloat16 [96, 384], replicated, may hold values from -0.3125 to 0.3125
- b_out: float32 [96], replicated, may hold values from -3 to 3
- layer_scale: float32 [96], replicated, may hold values from 0.4 to 1.2
Outputs:
- out_image: bfloat16 [4, 96, 1024, 128], P('slide', None, 'space')
- grad_image: bfloat16 [4, 96, 1024, 128], P('slide', None, 'space')
- grad_mlp: float32 [2, 96, 384], replicated
- grad_kernel: float32 [96, 49], replicated
- grad_vectors: float32 [5, 96], replicated
- grad_b_in: float32 [384], replicated
Inputs may be any that keep to these rules, and one draw needn't show every extreme that they name: In every slide, each of the 8 tiles of one index of space is either tissue or not.
All inputs are finite; a program needn't handle non-finite values.
Results may differ from a plain program's by a relative error of at most 0.007.
Values may be sent and summed in bfloat16 or wider, within the bound.
A program may use at most 64 MiB of HBM per device.

v0:
```python
import math

import jax
import jax.numpy as jnp
from jax import lax
from jax.sharding import PartitionSpec as P

TP = 16
TROWS = 8
TCOL_DEV = 1
MOST = 8


RADIUS = 3
KERNEL_SIDE = 7
EPSILON = 1e-06
GRAD_COEF = 4.0


def extended(block, sides, width):
    for axis, dim in sides:
        count = lax.axis_size(axis)
        forward = [(i, i + 1) for i in range(count - 1)]
        backward = [(target, source) for source, target in forward]
        low = lax.ppermute(
            lax.slice_in_dim(block, block.shape[dim] - width, None, axis=dim), axis, forward
        )
        high = lax.ppermute(lax.slice_in_dim(block, 0, width, axis=dim), axis, backward)
        block = jnp.concatenate([low, block, high], axis=dim)
    return block


def rounded(values):
    return lax.optimization_barrier(values.astype(jnp.bfloat16))


def gelu_value(values):
    return 0.5 * values * (1.0 + jax.scipy.special.erf(values * (1.0 / math.sqrt(2.0))))


def gelu_slope(values):
    return 0.5 * (1.0 + jax.scipy.special.erf(values * (1.0 / math.sqrt(2.0)))) + values * jnp.exp(
        -0.5 * values * values
    ) * (1.0 / math.sqrt(2.0 * math.pi))


def depthwise(padded, kernel, strip_w, strip_h):
    result = jnp.zeros((padded.shape[0], strip_w, strip_h), jnp.float32)
    for k_row in range(KERNEL_SIDE):
        for k_col in range(KERNEL_SIDE):
            weight = kernel[:, k_row * KERNEL_SIDE + k_col][:, None, None]
            result = result + weight * padded[
                :, k_row : k_row + strip_w, k_col : k_col + strip_h
            ].astype(jnp.float32)
    return result


def kernel_sums(padded, grad_pre, strip_w, strip_h):
    grad_f = grad_pre.astype(jnp.float32)
    entries = []
    for k_row in range(KERNEL_SIDE):
        for k_col in range(KERNEL_SIDE):
            piece = padded[:, k_row : k_row + strip_w, k_col : k_col + strip_h].astype(jnp.float32)
            entries.append(jnp.sum(grad_f * piece, axis=(1, 2)))
    return jnp.stack(entries, axis=1)


def to_tiles(planes):
    channels = planes.shape[0]
    shaped = planes.reshape(channels, TCOL_DEV, TP, TROWS, TP).transpose(1, 3, 0, 2, 4)
    return shaped.reshape(TCOL_DEV * TROWS, channels, TP * TP)


def from_tiles(tiles_in):
    channels = tiles_in.shape[1]
    shaped = tiles_in.reshape(TCOL_DEV, TROWS, channels, TP, TP).transpose(2, 0, 3, 1, 4)
    return shaped.reshape(channels, TCOL_DEV * TP, TROWS * TP)


def mlp_slots(w_in, w_out, b_in, b_out, x_slots, d_slots):
    flt = jnp.float32
    pre_act = (
        jnp.einsum("cf,scp->sfp", w_in, x_slots, preferred_element_type=flt) + b_in[None, :, None]
    )
    hidden = rounded(gelu_value(pre_act))
    mlp_out = rounded(
        jnp.einsum("cf,sfp->scp", w_out, hidden, preferred_element_type=flt) + b_out[None, :, None]
    )
    back_hid = jnp.einsum("cf,scp->sfp", w_out, d_slots, preferred_element_type=flt)
    grad_act = rounded(back_hid * gelu_slope(pre_act))
    grad_ln = rounded(jnp.einsum("cf,sfp->scp", w_in, grad_act, preferred_element_type=flt))
    gw_in = jnp.einsum("scp,sfp->cf", x_slots, grad_act, preferred_element_type=flt)
    gw_out = jnp.einsum("scp,sfp->cf", d_slots, hidden, preferred_element_type=flt)
    gb_in = jnp.sum(grad_act.astype(flt), axis=(0, 2))
    gb_out = jnp.sum(d_slots.astype(flt), axis=(0, 2))
    return (mlp_out, grad_ln, gw_in, gw_out, gb_in, gb_out)


def on_device(
    image,
    cotangent,
    tissue,
    dw_kernel,
    dw_bias,
    ln_gain,
    ln_bias,
    w_in,
    b_in,
    w_out,
    b_out,
    layer_scale,
):
    flt = jnp.float32
    strip_w = image.shape[2]
    strip_h = image.shape[3]
    gscale = GRAD_COEF / math.sqrt(
        lax.axis_size("space") * lax.axis_size("slide") * strip_w * strip_h
    )
    live_tiles = tissue[0]
    pixel_mask = jnp.repeat(jnp.repeat(live_tiles, TP, axis=0), TP, axis=1).astype(jnp.bfloat16)
    pix_f = pixel_mask[None].astype(flt)
    masked = image[0] * pixel_mask[None]
    rimmed = extended(masked, (("space", 1),), RADIUS)
    padded = jnp.pad(rimmed, ((0, 0), (0, 0), (RADIUS, RADIUS)))
    pre = depthwise(padded, dw_kernel, strip_w, strip_h) + dw_bias[:, None, None]
    centered = pre - jnp.mean(pre, axis=0, keepdims=True)
    inv_std = lax.rsqrt(jnp.mean(centered * centered, axis=0, keepdims=True) + EPSILON)
    normed = centered * inv_std
    ln_out = rounded(normed * ln_gain[:, None, None] + ln_bias[:, None, None])
    cot_f = cotangent[0].astype(flt)
    grad_mix = rounded(cot_f * pix_f * layer_scale[:, None, None])
    flat_live = live_tiles.reshape(-1)
    tile_count = flat_live.shape[0]
    tile_order = jnp.argsort((1 - flat_live) * tile_count + jnp.arange(tile_count, dtype=jnp.int32))
    own_x = to_tiles(ln_out)[tile_order]
    own_d = to_tiles(grad_mix)[tile_order]
    mo_slots, dxh_slots, gw_in, gw_out, gb_in, gb_out = mlp_slots(
        w_in, w_out, b_in, b_out, own_x, own_d
    )
    tile_rank = jnp.clip(jnp.cumsum(flat_live) - 1, 0, MOST - 1)
    keep_tile = flat_live.astype(jnp.bfloat16)[:, None, None]
    mlp_out = from_tiles(mo_slots[tile_rank] * keep_tile)
    grad_ln = from_tiles(dxh_slots[tile_rank] * keep_tile)
    out_image = (
        pix_f * (masked.astype(flt) + layer_scale[:, None, None] * mlp_out.astype(flt))
    ).astype(jnp.bfloat16)
    q_term = grad_ln.astype(flt) * ln_gain[:, None, None]
    grad_pre = rounded(
        inv_std
        * (
            q_term
            - jnp.mean(q_term, axis=0, keepdims=True)
            - normed * jnp.mean(q_term * normed, axis=0, keepdims=True)
        )
    )
    grad_rim = extended(grad_pre, (("space", 1),), RADIUS)
    grad_padded = jnp.pad(grad_rim, ((0, 0), (0, 0), (RADIUS, RADIUS)))
    back_conv = depthwise(grad_padded, dw_kernel[:, ::-1], strip_w, strip_h)
    grad_image = (pix_f * (cot_f + back_conv)).astype(jnp.bfloat16)
    grad_k = kernel_sums(padded, grad_pre, strip_w, strip_h) * gscale
    vectors = (
        jnp.stack(
            [
                jnp.sum(grad_pre.astype(flt), axis=(1, 2)),
                jnp.sum(grad_ln.astype(flt) * normed, axis=(1, 2)),
                jnp.sum(grad_ln.astype(flt), axis=(1, 2)),
                gb_out,
                jnp.sum(cot_f * pix_f * mlp_out.astype(flt), axis=(1, 2)),
            ],
            axis=0,
        )
        * gscale
    )
    local_mlp = jnp.stack([gw_in, gw_out], axis=0) * gscale
    grad_mlp, grad_kernel, grad_vectors, grad_b_in = lax.psum(
        (local_mlp, grad_k, vectors, gb_in * gscale), ("space", "slide")
    )
    return (out_image[None], grad_image[None], grad_mlp, grad_kernel, grad_vectors, grad_b_in)


def solution(mesh):
    placed = (
        P("slide", None, "space", None),
        P("slide", None, "space", None),
        P("slide", "space", None),
        P(),
        P(),
        P(),
        P(),
        P(),
        P(),
        P(),
        P(),
        P(),
    )
    return jax.shard_map(
        on_device,
        mesh=mesh,
        in_specs=placed,
        out_specs=(
            P("slide", None, "space", None),
            P("slide", None, "space", None),
            P(),
            P(),
            P(),
            P(),
        ),
        check_vma=False,
    )
```

profile of v0, /device:TPU:3, one launch (start us, length us, event | category | flops | bytes accessed | tf_op | source)
XLA Modules:
  0.0 348.4 jit_solution(11211395515160855288)
XLA Ops:
  7.3 1.4 copy.65
  8.7 0.7 convert_bitcast_fusion.2
  9.6 2.6 collective-permute-start.1
  12.2 3.4 collective-permute-start
  15.8 0.6 slice_bitcast_fusion.48
  16.5 0.7 slice_bitcast_fusion.47
  17.8 1.0 sort.17
  19.7 0.6 pad_clamp_fusion
  21.2 10.6 %fusion.163 = (f32[16,128]{1,0:T(8,128)S(1)}, f32[96,16,128]{0,2,1:T(8,128)S(1)}) fusion(f32[96]{0:T(128)} %param.16, bf16[96,22,134]{0,2,1:T(8,128)(2,1)S(1)} %select_maximum_fusion.2, f32[96]{0:T(128)S(1)} %get-tuple-element.141, f32[96]{0:T(128)S(1)} %get-tuple-element.142, f32[96]{0:T(128)S(1)} %get-tuple-element.95, bf16[96,3,128]{0,2,1:T(8,128)(2,1)} %copy-done.12, ...), kind=kLoop, calls=%fused_computation.379 | loop fusion | flops 30275584 | bytes 17869568 | tf_op jit(solution)/shard_map/reduce_sum | solution.py:126
  32.0 0.6 multiply_reduce_fusion.2
  32.7 0.6 add_convert_fusion
  33.3 0.8 copy.67
  34.2 2.5 gather_fusion
  36.6 3.5 %fusion.7 = (bf16[8,384,256]{1,2,0:T(8,128)(2,1)S(1)}, f32[8,256,384]{2,1,0:T(8,128)}) fusion(f32[384]{0:T(512)} %param.20, bf16[8,96,256]{1,2,0:T(8,128)(2,1)} %gather_fusion, bf16[96,384]{1,0:T(8,128)(2,1)S(1)} %copy-done), kind=kOutput, calls=%fused_computation.65 | convolution fusion | flops 155713536 | bytes 5187072 | tf_op jit(solution)/shard_map/cf,scp->sfp/dot_general | solution.py:83
  40.1 1.1 copy-done.4
  41.3 1.4 fusion.15
  42.6 2.4 gather_fusion.1
  45.1 2.0 copy.70
  47.1 1.2 convert_bitcast_fusion.1
  48.5 1.2 fusion.145
  49.7 0.9 fusion.17
  50.5 0.8 copy.73
  51.4 1.8 gather_fusion.2
  53.2 3.2 fusion.5
  56.5 1.1 copy-done.1
  57.6 1.4 fusion.14
  59.0 2.4 gather_fusion.3
  61.4 1.3 copy.76
  63.4 0.7 copy-done.5
  64.2 1.1 convolution_bitcast_fusion
  65.3 1.1 convolution_bitcast_fusion.1
  66.6 1.0 copy-done.6
  67.5 1.0 multiply_reduce_fusion
  68.7 2.3 multiply_convert_fusion
  71.0 1.1 fusion.140
  72.1 3.5 fusion.142
  75.6 3.2 fusion.141
  79.9 1.1 copy.84
  81.0 7.1 %collective-permute-start.3 = (bf16[96,3,128]{0,2,1:T(8,128)(2,1)S(1)}, bf16[96,3,128]{0,2,1:T(8,128)(2,1)S(1)}, u32[]{:S(2)}, u32[]{:S(2)}) collective-permute-start(bf16[96,3,128]{0,2,1:T(8,128)(2,1)S(1)} %get-tuple-element.91), channel_id=1, source_target_pairs={{4,0},{8,4},{12,8},{16,12},{20,16},{24,20},{28,24},{32,28},{36,32}... | collective-permute-start | bytes 221192 | tf_op jit(solution)/shard_map/ppermute | solution.py:28
  88.1 1.9 collective-permute-start.2
  90.1 0.7 maximum_multiply_fusion
  91.2 1.3 fusion.139
  92.7 0.7 stack.235
  93.4 79.7 %all-reduce.2 = (f32[96,49]{0,1:T(8,128)}, f32[5,96]{1,0:T(8,128)}, f32[384]{0:T(512)}) all-reduce(f32[96,49]{0,1:T(8,128)S(1)} %broadcast_multiply_fusion, f32[5,96]{1,0:T(8,128)S(1)} %broadcast_multiply_fusion.3, f32[384]{0:T(512)S(1)} %broadcast_multiply_fusion.4), channel_id=1, replica_groups=mesh['space'=64,'slide'=4] {'space','slide'}, use_global_device_ids=true, to_apply=%region_56.57 | all-reduce | flops 5568 | bytes 44544 | tf_op jit(solution)/shard_map/psum | solution.py:175
  173.8 10.4 %fusion.156 = bf16[1,96,16,128]{1,3,2,0:T(8,128)(2,1)S(1)} fusion(bf16[96,22,134]{0,2,1:T(8,128)(2,1)S(1)} %select_maximum_fusion, f32[96]{0:T(128)S(1)} %copy-done.49, f32[96]{0:T(128)S(1)} %copy-done.87, f32[96]{0:T(128)S(1)} %copy-done.27, bf16[96,3,128]{0,2,1:T(8,128)(2,1)S(1)} %collective-permute-done.3, ...), kind=kLoop, calls=%fused_computation.309 | loop fusion | flops 30670848 | bytes 17861504 | tf_op jit(solution)/shard_map/broadcast_in_dim | solution.py:178
  184.2 1.1 copy.85
  185.3 154.5 %all-reduce.5.cloned.1.call-done = f32[2,96,384]{2,1,0:T(8,128)} async-done(((f32[2,96,384]{2,1,0:T(8,128)}), f32[2,96,384]{2,1,0:T(8,128)}) %all-reduce.5.cloned.1.call-update) | async-done | bytes 294928 | tf_op jit(solution)/shard_map/psum | solution.py:175
  339.8 1.7 copy.95
  (274 shorter events, 5.2 us)
Async XLA Ops:
  7.2 29.5 %copy-start = (bf16[96,384]{1,0:T(8,128)(2,1)S(1)}, bf16[96,384]{1,0:T(8,128)(2,1)}, u32[]{:S(2)}) copy-start(bf16[96,384]{1,0:T(8,128)(2,1)} %param.19) | copy-start | bytes 221188
  7.2 332.6 %all-reduce.5.cloned.1.call-start = ((), (), s32[]{:S(2)}) async-start(), calls=%async_computation | async-start | bytes 589824 | tf_op jit(solution)/shard_map/psum | solution.py:175
  9.6 10.6 %collective-permute-start.1 = (bf16[96,3,128]{0,2,1:T(8,128)(2,1)S(1)}, bf16[96,3,128]{0,2,1:T(8,128)(2,1)S(1)}, u32[]{:S(2)}, u32[]{:S(2)}) collective-permute-start(bf16[96,3,128]{0,2,1:T(8,128)(2,1)S(1)} %get-tuple-element.93), channel_id=1, source_target_pairs={{4,0},{8,4},{12,8},{16,12},{20,16},{24,20},{28,24},{32,28},{36,32}... | collective-permute-start | bytes 221192 | tf_op jit(solution)/shard_map/ppermute | solution.py:28
  12.2 8.0 %collective-permute-start = (bf16[96,3,128]{0,2,1:T(8,128)(2,1)S(1)}, bf16[96,3,128]{0,2,1:T(8,128)(2,1)S(1)}, u32[]{:S(2)}, u32[]{:S(2)}) collective-permute-start(bf16[96,3,128]{0,2,1:T(8,128)(2,1)S(1)} %get-tuple-element.92), channel_id=1, source_target_pairs={{0,4},{4,8},{8,12},{12,16},{16,20},{20,24},{24,28},{28,32},{32,36}... | collective-permute-start | bytes 221192 | tf_op jit(solution)/shard_map/ppermute | solution.py:25
  15.7 16.1 %copy-start.26 = (f32[96]{0:T(128)}, f32[96]{0:T(128)S(1)}, u32[]{:S(2)}) copy-start(f32[96]{0:T(128)S(1)} %get-tuple-element.132) | copy-start | bytes 1156
  15.7 16.1 %copy-start.28 = (f32[96]{0:T(128)}, f32[96]{0:T(128)S(1)}, u32[]{:S(2)}) copy-start(f32[96]{0:T(128)S(1)} %get-tuple-element.133) | copy-start | bytes 1156
  81.0 92.2 %collective-permute-start.3 = (bf16[96,3,128]{0,2,1:T(8,128)(2,1)S(1)}, bf16[96,3,128]{0,2,1:T(8,128)(2,1)S(1)}, u32[]{:S(2)}, u32[]{:S(2)}) collective-permute-start(bf16[96,3,128]{0,2,1:T(8,128)(2,1)S(1)} %get-tuple-element.91), channel_id=1, source_target_pairs={{4,0},{8,4},{12,8},{16,12},{20,16},{24,20},{28,24},{32,28},{36,32}... | collective-permute-start | bytes 221192 | tf_op jit(solution)/shard_map/ppermute | solution.py:28
  88.1 85.0 %collective-permute-start.2 = (bf16[96,3,128]{0,2,1:T(8,128)(2,1)S(1)}, bf16[96,3,128]{0,2,1:T(8,128)(2,1)S(1)}, u32[]{:S(2)}, u32[]{:S(2)}) collective-permute-start(bf16[96,3,128]{0,2,1:T(8,128)(2,1)S(1)} %get-tuple-element.90), channel_id=1, source_target_pairs={{0,4},{4,8},{8,12},{12,16},{16,20},{20,24},{24,28},{28,32},{32,36}... | collective-permute-start | bytes 221192 | tf_op jit(solution)/shard_map/ppermute | solution.py:25
  90.8 82.6 %copy-start.25 = (f32[128]{0:T(128)S(1)}, f32[128]{0:T(128)}, u32[]{:S(2)}) copy-start(f32[128]{0:T(128)} %convert_element_type.466) | copy-start | bytes 1540
  90.9 82.6 %copy-start.27 = (f32[96]{0:T(128)S(1)}, f32[96]{0:T(128)}, u32[]{:S(2)}) copy-start(f32[96]{0:T(128)} %copy-done.26) | copy-start | bytes 1156
  90.9 82.6 %copy-start.29 = (f32[96]{0:T(128)S(1)}, f32[96]{0:T(128)}, u32[]{:S(2)}) copy-start(f32[96]{0:T(128)} %copy-done.28) | copy-start | bytes 1156
  90.9 82.6 %copy-start.31 = (f32[96]{0:T(128)S(1)}, f32[96]{0:T(128)}, u32[]{:S(2)}) copy-start(f32[96]{0:T(128)} %copy-done.30) | copy-start | bytes 1156
  90.9 82.6 %copy-start.33 = (f32[96]{0:T(128)S(1)}, f32[96]{0:T(128)}, u32[]{:S(2)}) copy-start(f32[96]{0:T(128)} %copy-done.32) | copy-start | bytes 1156
  90.9 82.6 %copy-start.35 = (f32[96]{0:T(128)S(1)}, f32[96]{0:T(128)}, u32[]{:S(2)}) copy-start(f32[96]{0:T(128)} %copy-done.34) | copy-start | bytes 1156
  90.9 82.6 %copy-start.37 = (f32[96]{0:T(128)S(1)}, f32[96]{0:T(128)}, u32[]{:S(2)}) copy-start(f32[96]{0:T(128)} %copy-done.36) | copy-start | bytes 1156
  90.9 82.6 %copy-start.39 = (f32[96]{0:T(128)S(1)}, f32[96]{0:T(128)}, u32[]{:S(2)}) copy-start(f32[96]{0:T(128)} %copy-done.38) | copy-start | bytes 1156
  90.9 82.6 %copy-start.41 = (f32[96]{0:T(128)S(1)}, f32[96]{0:T(128)}, u32[]{:S(2)}) copy-start(f32[96]{0:T(128)} %copy-done.40) | copy-start | bytes 1156
  90.9 82.6 %copy-start.43 = (f32[96]{0:T(128)S(1)}, f32[96]{0:T(128)}, u32[]{:S(2)}) copy-start(f32[96]{0:T(128)} %copy-done.42) | copy-start | bytes 1156
  90.9 82.6 %copy-start.45 = (f32[96]{0:T(128)S(1)}, f32[96]{0:T(128)}, u32[]{:S(2)}) copy-start(f32[96]{0:T(128)} %copy-done.44) | copy-start | bytes 1156
  91.0 82.6 %copy-start.47 = (f32[96]{0:T(128)S(1)}, f32[96]{0:T(128)}, u32[]{:S(2)}) copy-start(f32[96]{0:T(128)} %copy-done.46) | copy-start | bytes 1156
  91.0 82.6 %copy-start.49 = (f32[96]{0:T(128)S(1)}, f32[96]{0:T(128)}, u32[]{:S(2)}) copy-start(f32[96]{0:T(128)} %copy-done.48) | copy-start | bytes 1156
  91.0 82.6 %copy-start.51 = (f32[96]{0:T(128)S(1)}, f32[96]{0:T(128)}, u32[]{:S(2)}) copy-start(f32[96]{0:T(128)} %copy-done.50) | copy-start | bytes 1156
  91.0 82.6 %copy-start.53 = (f32[96]{0:T(128)S(1)}, f32[96]{0:T(128)}, u32[]{:S(2)}) copy-start(f32[96]{0:T(128)} %copy-done.52) | copy-start | bytes 1156
  91.0 82.6 %copy-start.55 = (f32[96]{0:T(128)S(1)}, f32[96]{0:T(128)}, u32[]{:S(2)}) copy-start(f32[96]{0:T(128)} %copy-done.54) | copy-start | bytes 1156
  91.0 82.6 %copy-start.57 = (f32[96]{0:T(128)S(1)}, f32[96]{0:T(128)}, u32[]{:S(2)}) copy-start(f32[96]{0:T(128)} %copy-done.56) | copy-start | bytes 1156
  91.0 82.6 %copy-start.59 = (f32[96]{0:T(128)S(1)}, f32[96]{0:T(128)}, u32[]{:S(2)}) copy-start(f32[96]{0:T(128)} %copy-done.58) | copy-start | bytes 1156
  91.0 82.6 %copy-start.61 = (f32[96]{0:T(128)S(1)}, f32[96]{0:T(128)}, u32[]{:S(2)}) copy-start(f32[96]{0:T(128)} %copy-done.60) | copy-start | bytes 1156
  91.0 82.6 %copy-start.63 = (f32[96]{0:T(128)S(1)}, f32[96]{0:T(128)}, u32[]{:S(2)}) copy-start(f32[96]{0:T(128)} %copy-done.62) | copy-start | bytes 1156
  91.0 82.6 %copy-start.65 = (f32[96]{0:T(128)S(1)}, f32[96]{0:T(128)}, u32[]{:S(2)}) copy-start(f32[96]{0:T(128)} %copy-done.64) | copy-start | bytes 1156
  91.1 82.6 %copy-start.67 = (f32[96]{0:T(128)S(1)}, f32[96]{0:T(128)}, u32[]{:S(2)}) copy-start(f32[96]{0:T(128)} %get-tuple-element.103) | copy-start | bytes 1156
  91.1 82.6 %copy-start.69 = (f32[96]{0:T(128)S(1)}, f32[96]{0:T(128)}, u32[]{:S(2)}) copy-start(f32[96]{0:T(128)} %get-tuple-element.104) | copy-start | bytes 1156
  91.1 82.6 %copy-start.71 = (f32[96]{0:T(128)S(1)}, f32[96]{0:T(128)}, u32[]{:S(2)}) copy-start(f32[96]{0:T(128)} %get-tuple-element.105) | copy-start | bytes 1156
  91.1 82.6 %copy-start.73 = (f32[96]{0:T(128)S(1)}, f32[96]{0:T(128)}, u32[]{:S(2)}) copy-start(f32[96]{0:T(128)} %get-tuple-element.106) | copy-start | bytes 1156
  91.1 82.6 %copy-start.75 = (f32[96]{0:T(128)S(1)}, f32[96]{0:T(128)}, u32[]{:S(2)}) copy-start(f32[96]{0:T(128)} %get-tuple-element.107) | copy-start | bytes 1156
  91.1 82.6 %copy-start.77 = (f32[96]{0:T(128)S(1)}, f32[96]{0:T(128)}, u32[]{:S(2)}) copy-start(f32[96]{0:T(128)} %get-tuple-element.108) | copy-start | bytes 1156
  91.1 82.6 %copy-start.79 = (f32[96]{0:T(128)S(1)}, f32[96]{0:T(128)}, u32[]{:S(2)}) copy-start(f32[96]{0:T(128)} %get-tuple-element.109) | copy-start | bytes 1156
  91.1 82.6 %copy-start.81 = (f32[96]{0:T(128)S(1)}, f32[96]{0:T(128)}, u32[]{:S(2)}) copy-start(f32[96]{0:T(128)} %get-tuple-element.110) | copy-start | bytes 1156
  91.1 82.6 %copy-start.83 = (f32[96]{0:T(128)S(1)}, f32[96]{0:T(128)}, u32[]{:S(2)}) copy-start(f32[96]{0:T(128)} %get-tuple-element.111) | copy-start | bytes 1156
  91.1 82.6 %copy-start.85 = (f32[96]{0:T(128)S(1)}, f32[96]{0:T(128)}, u32[]{:S(2)}) copy-start(f32[96]{0:T(128)} %get-tuple-element.112) | copy-start | bytes 1156
  91.2 82.6 %copy-start.87 = (f32[96]{0:T(128)S(1)}, f32[96]{0:T(128)}, u32[]{:S(2)}) copy-start(f32[96]{0:T(128)} %get-tuple-element.113) | copy-start | bytes 1156
  91.2 82.6 %copy-start.89 = (f32[96]{0:T(128)S(1)}, f32[96]{0:T(128)}, u32[]{:S(2)}) copy-start(f32[96]{0:T(128)} %get-tuple-element.114) | copy-start | bytes 1156
  91.2 82.6 %copy-start.91 = (f32[96]{0:T(128)S(1)}, f32[96]{0:T(128)}, u32[]{:S(2)}) copy-start(f32[96]{0:T(128)} %get-tuple-element.115) | copy-start | bytes 1156
  91.2 82.6 %copy-start.93 = (f32[96]{0:T(128)S(1)}, f32[96]{0:T(128)}, u32[]{:S(2)}) copy-start(f32[96]{0:T(128)} %get-tuple-element.116) | copy-start | bytes 1156
  91.2 82.6 %copy-start.95 = (f32[96]{0:T(128)S(1)}, f32[96]{0:T(128)}, u32[]{:S(2)}) copy-start(f32[96]{0:T(128)} %get-tuple-element.117) | copy-start | bytes 1156
  91.2 82.6 %copy-start.97 = (f32[96]{0:T(128)S(1)}, f32[96]{0:T(128)}, u32[]{:S(2)}) copy-start(f32[96]{0:T(128)} %get-tuple-element.118) | copy-start | bytes 1156
  91.2 82.6 %copy-start.99 = (f32[96]{0:T(128)S(1)}, f32[96]{0:T(128)}, u32[]{:S(2)}) copy-start(f32[96]{0:T(128)} %get-tuple-element.119) | copy-start | bytes 1156
  92.5 81.3 %copy-start.101 = (f32[96]{0:T(128)S(1)}, f32[96]{0:T(128)}, u32[]{:S(2)}) copy-start(f32[96]{0:T(128)} %get-tuple-element.120) | copy-start | bytes 1156
  92.6 81.3 %copy-start.103 = (f32[96]{0:T(128)S(1)}, f32[96]{0:T(128)}, u32[]{:S(2)}) copy-start(f32[96]{0:T(128)} %get-tuple-element.121) | copy-start | bytes 1156
  (77 other events, 495.7 us)
Sparse Core Ops, SparseCore 0:
  90.9 248.8 all-reduce.4
where the time goes:
time: 350 us; the launch traced here: 348 us
  waiting for transfers between devices  155 us (44%)
  blocking collectives  79.7 us (23%)
  other arithmetic  43.6 us (12%)
  local copies, waits for them, and re-layouts  27.7 us (8%)
  between operations  16 us (5%)
  starting transfers between devices  15.1 us (4%)
  matrix products  11.7 us (3%)
    psum x1, waiting for transfers between devices, on_device(): lax.psum((local_mlp, grad_k, vectors, gb_in * gscale), ('space', 'slide'))  155 us
    psum x1, blocking collectives, on_device(): lax.psum((local_mlp, grad_k, vectors, gb_in * gscale), ('space', 'slide'))  79.7 us
    unnamed x245, local copies, waits for them, and re-layouts  11 us
    reduce_sum x1, other arithmetic, on_device(): centered = pre - jnp.mean(pre, axis=0, keepdims=True)  10.6 us
    broadcast_in_dim x1, other arithmetic, on_device(): grad_image[None]  10.4 us
    ppermute x2, starting transfers between devices, extended(): lax.ppermute(lax.slice_in_dim(block, 0, width, axis=dim), axis, backward)  9.73 us
    reduce_sum x4, other arithmetic, kernel_sums(): entries.append(jnp.sum(grad_f * piece, axis=(1, 2)))  9.1 us
  transfers between devices with their start and end apart: 5, of which 1 were waited for; matrix products, arithmetic and copies ran while one was open for 5% of the time, Pallas kernels for 0%

commit v1 on v0

--- a/solution.py
+++ b/solution.py
@@ -28,6 +28,47 @@
         high = lax.ppermute(lax.slice_in_dim(block, 0, width, axis=dim), axis, backward)
         block = jnp.concatenate([low, block, high], axis=dim)
     return block
+
+
+def exchanged(values, axis, stride):
+    count = lax.axis_size(axis)
+    return lax.ppermute(values, axis, [(i, i ^ stride) for i in range(count)])
+
+
+def summed_everywhere(parts, axes, lanes=128):
+    flat = jnp.concatenate([p.reshape(-1) for p in parts])
+    rows = -(-flat.shape[0] // lanes)
+    rows += (-rows) % 128
+    block = jnp.pad(flat, (0, rows * lanes - flat.shape[0])).reshape(rows, lanes)
+    steps = []
+    for axis in axes:
+        stride = 1
+        while stride < lax.axis_size(axis):
+            height = block.shape[0]
+            if height % 2:
+                block = block + exchanged(block, axis, stride)
+                steps.append((axis, stride, None))
+            else:
+                half = height // 2
+                upper = (lax.axis_index(axis) // stride) % 2 == 1
+                keep = jnp.where(upper, block[half:], block[:half])
+                send = jnp.where(upper, block[:half], block[half:])
+                block = keep + exchanged(send, axis, stride)
+                steps.append((axis, stride, upper))
+            stride *= 2
+    for axis, stride, upper in reversed(steps):
+        if upper is None:
+            continue
+        got = exchanged(block, axis, stride)
+        block = jnp.where(
+            upper, jnp.concatenate([got, block]), jnp.concatenate([block, got])
+        )
+    flat = block.reshape(-1)
+    out, start = [], 0
+    for p in parts:
+        out.append(flat[start : start + p.size].reshape(p.shape))
+        start += p.size
+    return tuple(out)
 
 
 def rounded(values):
@@ -172,7 +213,7 @@
         * gscale
     )
     local_mlp = jnp.stack([gw_in, gw_out], axis=0) * gscale
-    grad_mlp, grad_kernel, grad_vectors, grad_b_in = lax.psum(
+    grad_mlp, grad_kernel, grad_vectors, grad_b_in = summed_everywhere(
         (local_mlp, grad_k, vectors, gb_in * gscale), ("space", "slide")
     )
     return (out_image[None], grad_image[None], grad_mlp, grad_kernel, grad_vectors, grad_b_in)

time: 350 us -> 168 us (0.48)
  waiting for transfers between devices: 155 us -> 35.7 us
  blocking collectives: 79.7 us -> 0 us
  starting transfers between devices: 15.1 us -> 43.2 us
  between operations: 16 us -> 2.62 us
    psum x1 -> x0, waiting for transfers between devices: 155 us -> none  [on_device(): lax.psum((local_mlp, grad_k, vectors, gb_in * gscale), ('space', 'slide'))]
    psum x1 -> x0, blocking collectives: 79.7 us -> none  [on_device(): lax.psum((local_mlp, grad_k, vectors, gb_in * gscale), ('space', 'slide'))]
    ppermute x0 -> x15, waiting for transfers between devices: none -> 34.5 us  [exchanged(): return lax.ppermute(values, axis, [(i, i ^ stride) for i in range(count)])]
    ppermute x0 -> x15, starting transfers between devices: none -> 21.4 us  [exchanged(): return lax.ppermute(values, axis, [(i, i ^ stride) for i in range(count)])]
    ppermute x2, starting transfers between devices: 9.73 us -> 16.4 us  [extended(): lax.ppermute(lax.slice_in_dim(block, 0, width, axis=dim), axis, backward)]
    unnamed x245 -> x219, local copies, waits for them, and re-layouts: 11 us -> 8.43 us
  transfers between devices with their start and end apart: 5 -> 19, of which waited for: 1 -> 14; matrix products, arithmetic and copies ran while one was open for 5% -> 10% of each run, Pallas kernels for 0% -> 0%
where the time goes in v1:
time: 168 us; the launch traced here: 167 us
  other arithmetic  45.1 us (27%)
  starting transfers between devices  43.2 us (26%)
  waiting for transfers between devices  35.7 us (21%)
  local copies, waits for them, and re-layouts  30.1 us (18%)
  matrix products  10.3 us (6%)
  between operations  2.62 us (2%)
    ppermute x15, waiting for transfers between devices, exchanged(): return lax.ppermute(values, axis, [(i, i ^ stride) for i in range(count)])  34.5 us
    ppermute x15, starting transfers between devices, exchanged(): return lax.ppermute(values, axis, [(i, i ^ stride) for i in range(count)])  21.4 us
    ppermute x2, starting transfers between devices, extended(): lax.ppermute(lax.slice_in_dim(block, 0, width, axis=dim), axis, backward)  16.4 us
    reduce_sum x1, other arithmetic, on_device(): centered = pre - jnp.mean(pre, axis=0, keepdims=True)  10.4 us
    broadcast_in_dim x1, other arithmetic, on_device(): grad_image[None]  10.4 us
    reduce_sum x4, other arithmetic, kernel_sums(): entries.append(jnp.sum(grad_f * piece, axis=(1, 2)))  9.09 us
    unnamed x219, local copies, waits for them, and re-layouts  8.43 us
    ppermute x2, starting transfers between devices, extended(): lax.ppermute(lax.slice_in_dim(block, block.shape[dim] - width, None, axis...  5.36 us
  transfers between devices with their start and end apart: 19, of which 14 were waited for; matrix products, arithmetic and copies ran while one was open for 10% of the time, Pallas kernels for 0%

profile of v1, /device:TPU:3, one launch (start us, length us, event | category | flops | bytes accessed | tf_op | source)
XLA Modules:
  0.0 167.0 jit_solution(144543447639277550)
XLA Ops:
  0.7 1.4 copy.69
  4.3 2.6 %collective-permute-start.1 = (bf16[96,3,128]{0,2,1:T(8,128)(2,1)S(1)}, bf16[96,3,128]{0,2,1:T(8,128)(2,1)S(1)}, u32[]{:S(2)}, u32[]{:S(2)}) collective-permute-start(bf16[96,3,128]{0,2,1:T(8,128)(2,1)S(1)} %get-tuple-element.90), channel_id=1, source_target_pairs={{4,0},{8,4},{12,8},{16,12},{20,16},{24,20},{28,24},{32,28},{36,32}... | collective-permute-start | bytes 221192 | tf_op jit(solution)/shard_map/ppermute | solution.py:28
  6.9 3.4 %collective-permute-start = (bf16[96,3,128]{0,2,1:T(8,128)(2,1)S(1)}, bf16[96,3,128]{0,2,1:T(8,128)(2,1)S(1)}, u32[]{:S(2)}, u32[]{:S(2)}) collective-permute-start(bf16[96,3,128]{0,2,1:T(8,128)(2,1)S(1)} %get-tuple-element.89), channel_id=1, source_target_pairs={{0,4},{4,8},{8,12},{12,16},{16,20},{20,24},{24,28},{28,32},{32,36}... | collective-permute-start | bytes 221192 | tf_op jit(solution)/shard_map/ppermute | solution.py:25
  13.6 1.2 collective-permute-done
  15.1 10.4 %fusion.164 = (f32[16,128]{1,0:T(8,128)S(1)}, f32[96,16,128]{0,2,1:T(8,128)S(1)}) fusion(f32[96]{0:T(128)S(1)} %copy-done.103, bf16[96,22,134]{0,2,1:T(8,128)(2,1)S(1)} %select_maximum_fusion.2, f32[96]{0:T(128)S(1)} %get-tuple-element.138, f32[96]{0:T(128)S(1)} %get-tuple-element.139, f32[96]{0:T(128)S(1)} %get-tuple-element.92, ...), kind=kLoop, calls=%fused_computation.402 | loop fusion | flops 30275584 | bytes 17869568 | tf_op jit(solution)/shard_map/reduce_sum | solution.py:167
  28.0 2.5 %gather_fusion = bf16[8,96,256]{1,2,0:T(8,128)(2,1)} fusion(bf16[8,96,256]{1,2,0:T(8,128)(2,1)} %bitcast.260, s32[1024]{0:T(1024)S(1)} %pad_clamp_fusion.1), kind=kCustom, calls=%fused_computation | custom fusion | bytes 786464 | tf_op jit(solution)/shard_map/gather | solution.py:176
  30.5 3.5 %fusion.7 = (bf16[8,384,256]{1,2,0:T(8,128)(2,1)S(1)}, f32[8,256,384]{2,1,0:T(8,128)}) fusion(f32[384]{0:T(512)S(1)} %copy-done.97, bf16[8,96,256]{1,2,0:T(8,128)(2,1)} %gather_fusion, bf16[96,384]{1,0:T(8,128)(2,1)S(1)} %copy-done), kind=kOutput, calls=%fused_computation.65 | convolution fusion | flops 155713536 | bytes 5187072 | tf_op jit(solution)/shard_map/cf,scp->sfp/dot_general | solution.py:124
  34.0 1.1 copy-done.4
  35.1 1.4 fusion.15
  36.5 2.3 %gather_fusion.1 = bf16[8,96,256]{2,1,0:T(8,128)(2,1)} fusion(bf16[8,96,256]{2,1,0:T(8,128)(2,1)} %fusion.15, s32[1024]{0:T(1024)S(1)} %pad_clamp_fusion), kind=kCustom, calls=%fused_computation.1 | custom fusion | bytes 786464 | tf_op jit(solution)/shard_map/gather | solution.py:183
  38.8 2.0 %copy.74 = bf16[8,96,256]{1,2,0:T(8,128)(2,1)} copy(bf16[8,96,256]{2,1,0:T(8,128)(2,1)} %gather_fusion.1) | data formatting | bytes 786432 | tf_op jit(solution)/shard_map/gather | solution.py:183
  40.8 1.2 convert_bitcast_fusion.1
  43.9 1.7 %gather_fusion.2 = bf16[8,96,256]{1,2,0:T(8,128)(2,1)S(1)} fusion(bf16[8,96,256]{1,2,0:T(8,128)(2,1)} %bitcast.259, s32[1024]{0:T(1024)S(1)} %pad_clamp_fusion.1), kind=kCustom, calls=%fused_computation.2 | custom fusion | bytes 786464 | tf_op jit(solution)/shard_map/gather | solution.py:177
  45.6 3.2 %fusion.5 = bf16[8,384,256]{1,2,0:T(8,128)(2,1)S(1)} fusion(f32[8,256,384]{2,1,0:T(8,128)} %get-tuple-element.141, bf16[8,96,256]{1,2,0:T(8,128)(2,1)S(1)} %gather_fusion.2, f32[384]{0:T(512)S(1)} %copy-done.97, bf16[96,384]{1,0:T(8,128)(2,1)S(1)} %copy-done.20), kind=kOutput, calls=%fused_computation.61 | convolution fusion | flops 159645696 | bytes 5187072 | tf_op jit(solution)/shard_map/cf,scp->sfp/dot_general | solution.py:130
  48.9 1.1 copy-done.1
  50.0 1.4 fusion.14
  51.4 2.3 %gather_fusion.3 = bf16[8,96,256]{2,1,0:T(8,128)(2,1)} fusion(bf16[8,96,256]{2,1,0:T(8,128)(2,1)} %fusion.14, s32[1024]{0:T(1024)S(1)} %pad_clamp_fusion), kind=kCustom, calls=%fused_computation.3 | custom fusion | bytes 786464 | tf_op jit(solution)/shard_map/gather | solution.py:184
  53.7 1.3 copy.80
  56.1 1.1 convert_reduce_fusion.2
  59.0 1.3 copy.81
  61.3 1.5 multiply_reduce_fusion
  63.0 2.3 %multiply_convert_fusion = bf16[96,16,128]{0,2,1:T(8,128)(2,1)S(1)} fusion(f32[96,16,128]{0,2,1:T(8,128)} %bitcast.253, f32[96,16,128]{0,2,1:T(8,128)S(1)} %get-tuple-element.84, f32[16,128]{1,0:T(8,128)S(1)} %broadcast_multiply_fusion.1, f32[16,128]{1,0:T(8,128)S(1)} %div.58, f32[96]{0:T(128)S(1)} %copy-done.22, f32[16,128]{1,0:T(8,128)S(1)} %add_rsqrt_fusion, ...), kind=kLoop, calls=%fused_computation.269 | loop fusion | flops 1572864 | bytes 1999232 | tf_op jit(solution)/shard_map/convert_element_type | solution.py:75
  66.4 3.5 %fusion.142 = (f32[96]{0:T(128)S(1)}, f32[96]{0:T(128)S(1)}, f32[96]{0:T(128)S(1)}, f32[96]{0:T(128)S(1)}, f32[96]{0:T(128)S(1)}, /*index=5*/f32[96]{0:T(128)S(1...) fusion(bf16[96,16,128]{0,2,1:T(8,128)(2,1)S(1)} %multiply_conve, ...), kind=kLoop, calls=%fused_computation.261 | loop fusion | flops 10811712 | bytes 7478016 | tf_op jit(solution)/shard_map/reduce_sum | solution.py:105
  69.9 3.2 %fusion.141 = (f32[96]{0:T(128)S(1)}, f32[96]{0:T(128)S(1)}, f32[96]{0:T(128)S(1)}, f32[96]{0:T(128)S(1)}, f32[96]{0:T(128)S(1)}, /*index=5*/f32[96]{0:T(128)S(1...) fusion(bf16[96,16,128]{0,2,1:T(8,128)(2,1)S(1)} %multiply_conve, ...), kind=kLoop, calls=%fused_computation.260 | loop fusion | flops 10811712 | bytes 7478016 | tf_op jit(solution)/shard_map/reduce_sum | solution.py:105
  73.8 1.3 fusion.139
  75.7 1.4 concatenate.77
  77.1 5.4 %collective-permute-start.4 = (f32[320,128]{1,0:T(8,128)S(1)}, f32[320,128]{1,0:T(8,128)S(1)}, u32[]{:S(2)}, u32[]{:S(2)}) collective-permute-start(f32[320,128]{1,0:T(8,128)S(1)} %slice_select_fusion), channel_id=1, source_target_pairs={{0,4},{4,0},{8,12},{12,8},{16,20},{20,16},{24,28},{28,24},{32,36},... | collective-permute-start | bytes 491528 | tf_op jit(solution)/shard_map/ppermute | solution.py:35
  83.8 3.6 %collective-permute-done.5 = f32[160,128]{1,0:T(8,128)S(1)} collective-permute-done((f32[160,128]{1,0:T(8,128)S(1)}, f32[160,128]{1,0:T(8,128)S(1)}, u32[]{:S(2)}, u32[]{:S(2)}) %collective-permute-start.5) | collective-permute-done | bytes 81952 | tf_op jit(solution)/shard_map/ppermute | solution.py:35
  87.5 4.1 %collective-permute-done.6 = f32[80,128]{1,0:T(8,128)S(1)} collective-permute-done((f32[80,128]{1,0:T(8,128)S(1)}, f32[80,128]{1,0:T(8,128)S(1)}, u32[]{:S(2)}, u32[]{:S(2)}) %collective-permute-start.6) | collective-permute-done | bytes 40992 | tf_op jit(solution)/shard_map/ppermute | solution.py:35
  92.3 6.0 %collective-permute-done.7 = f32[40,128]{1,0:T(8,128)S(1)} collective-permute-done((f32[40,128]{1,0:T(8,128)S(1)}, f32[40,128]{1,0:T(8,128)S(1)}, u32[]{:S(2)}, u32[]{:S(2)}) %collective-permute-start.7) | collective-permute-done | bytes 20512 | tf_op jit(solution)/shard_map/ppermute | solution.py:35
  98.5 2.7 %collective-permute-done.8 = f32[20,128]{1,0:T(8,128)S(1)} collective-permute-done((f32[20,128]{1,0:T(8,128)S(1)}, f32[20,128]{1,0:T(8,128)S(1)}, u32[]{:S(2)}, u32[]{:S(2)}) %collective-permute-start.8) | collective-permute-done | bytes 10272 | tf_op jit(solution)/shard_map/ppermute | solution.py:35
  101.2 2.2 %collective-permute-start.9 = (f32[10,128]{1,0:T(8,128)S(1)}, f32[10,128]{1,0:T(8,128)S(1)}, u32[]{:S(2)}, u32[]{:S(2)}) collective-permute-start(f32[10,128]{1,0:T(8,128)S(1)} %slice_select_fusion.5), channel_id=1, source_target_pairs={{0,128},{4,132},{8,136},{12,140},{16,144},{20,148},{24,152},{28,15... | collective-permute-start | bytes 15368 | tf_op jit(solution)/shard_map/ppermute | solution.py:35
  103.4 1.8 %collective-permute-done.9 = f32[10,128]{1,0:T(8,128)S(1)} collective-permute-done((f32[10,128]{1,0:T(8,128)S(1)}, f32[10,128]{1,0:T(8,128)S(1)}, u32[]{:S(2)}, u32[]{:S(2)}) %collective-permute-start.9) | collective-permute-done | bytes 5152 | tf_op jit(solution)/shard_map/ppermute | solution.py:35
  105.3 1.4 collective-permute-start.10
  106.7 1.2 collective-permute-done.10
  107.8 2.9 %collective-permute-start.11 = (f32[5,128]{1,0:T(8,128)S(1)}, f32[5,128]{1,0:T(8,128)S(1)}, u32[]{:S(2)}, u32[]{:S(2)}) collective-permute-start(f32[5,128]{1,0:T(8,128)S(1)} %select_add_fusion.6), channel_id=1, source_target_pairs={{0,2},{1,3},{2,0},{3,1},{4,6},{5,7},{6,4},{7,5},{8,10},{9,11},{10,... | collective-permute-start | bytes 7688 | tf_op jit(solution)/shard_map/ppermute | solution.py:35
  111.8 1.3 collective-permute-start.12
  113.1 1.2 collective-permute-done.12
  114.3 2.2 %collective-permute-start.13 = (f32[10,128]{1,0:T(8,128)S(1)}, f32[10,128]{1,0:T(8,128)S(1)}, u32[]{:S(2)}, u32[]{:S(2)}) collective-permute-start(f32[10,128]{1,0:T(8,128)S(1)} %maximum_select_fusion.6), channel_id=1, source_target_pairs={{0,128},{4,132},{8,136},{12,140},{16,144},{20,148},{24,152},{28,15... | collective-permute-start | bytes 15368 | tf_op jit(solution)/shard_map/ppermute | solution.py:35
  116.5 2.1 %collective-permute-done.13 = f32[10,128]{1,0:T(8,128)S(1)} collective-permute-done((f32[10,128]{1,0:T(8,128)S(1)}, f32[10,128]{1,0:T(8,128)S(1)}, u32[]{:S(2)}, u32[]{:S(2)}) %collective-permute-start.13) | collective-permute-done | bytes 5152 | tf_op jit(solution)/shard_map/ppermute | solution.py:35
  118.8 2.5 %collective-permute-done.14 = f32[20,128]{1,0:T(8,128)S(1)} collective-permute-done((f32[20,128]{1,0:T(8,128)S(1)}, f32[20,128]{1,0:T(8,128)S(1)}, u32[]{:S(2)}, u32[]{:S(2)}) %collective-permute-start.14) | collective-permute-done | bytes 10272 | tf_op jit(solution)/shard_map/ppermute | solution.py:35
  122.2 1.1 fusion.145
  123.4 4.8 %collective-permute-done.15 = f32[40,128]{1,0:T(8,128)S(1)} collective-permute-done((f32[40,128]{1,0:T(8,128)S(1)}, f32[40,128]{1,0:T(8,128)S(1)}, u32[]{:S(2)}, u32[]{:S(2)}) %collective-permute-start.15) | collective-permute-done | bytes 20512 | tf_op jit(solution)/shard_map/ppermute | solution.py:35
  129.8 13.8 %collective-permute-start.3 = (bf16[96,3,128]{0,2,1:T(8,128)(2,1)S(1)}, bf16[96,3,128]{0,2,1:T(8,128)(2,1)S(1)}, u32[]{:S(2)}, u32[]{:S(2)}) collective-permute-start(bf16[96,3,128]{0,2,1:T(8,128)(2,1)S(1)} %get-tuple-element.88), channel_id=1, source_target_pairs={{4,0},{8,4},{12,8},{16,12},{20,16},{24,20},{28,24},{32,28},{36,32}... | collective-permute-start | bytes 221192 | tf_op jit(solution)/shard_map/ppermute | solution.py:28
  143.6 1.9 %collective-permute-start.2 = (bf16[96,3,128]{0,2,1:T(8,128)(2,1)S(1)}, bf16[96,3,128]{0,2,1:T(8,128)(2,1)S(1)}, u32[]{:S(2)}, u32[]{:S(2)}) collective-permute-start(bf16[96,3,128]{0,2,1:T(8,128)(2,1)S(1)} %get-tuple-element.87), channel_id=1, source_target_pairs={{0,4},{4,8},{8,12},{12,16},{16,20},{20,24},{24,28},{28,32},{32,36}... | collective-permute-start | bytes 221192 | tf_op jit(solution)/shard_map/ppermute | solution.py:25
  145.6 2.9 %collective-permute-start.17 = (f32[160,128]{1,0:T(8,128)S(1)}, f32[160,128]{1,0:T(8,128)S(1)}, u32[]{:S(2)}, u32[]{:S(2)}) collective-permute-start(f32[160,128]{1,0:T(8,128)S(1)} %maximum_select_fusion.2), channel_id=1, source_target_pairs={{0,8},{4,12},{8,0},{12,4},{16,24},{20,28},{24,16},{28,20},{32,40},... | collective-permute-start | bytes 245768 | tf_op jit(solution)/shard_map/ppermute | solution.py:35
  148.7 2.4 %collective-permute-done.17 = f32[160,128]{1,0:T(8,128)S(1)} collective-permute-done((f32[160,128]{1,0:T(8,128)S(1)}, f32[160,128]{1,0:T(8,128)S(1)}, u32[]{:S(2)}, u32[]{:S(2)}) %collective-permute-start.17) | collective-permute-done | bytes 81952 | tf_op jit(solution)/shard_map/ppermute | solution.py:35
  152.4 10.4 %fusion.156 = bf16[1,96,16,128]{1,3,2,0:T(8,128)(2,1)S(1)} fusion(bf16[96,22,134]{0,2,1:T(8,128)(2,1)S(1)} %select_maximum_fusion, f32[96]{0:T(128)S(1)} %copy-done.34, f32[96]{0:T(128)S(1)} %copy-done.72, f32[96]{0:T(128)S(1)} %get-tuple-element.129, bf16[96,3,128]{0,2,1:T(8,128)(2,1)S(1)} %collective-permute-done.3, ...), kind=kLoop, calls=%fused_computation.309 | loop fusion | flops 30670848 | bytes 17861504 | tf_op jit(solution)/shard_map/broadcast_in_dim | solution.py:219
  (309 shorter events, 26.5 us)
Async XLA Ops:
  0.6 29.8 %copy-start = (bf16[96,384]{1,0:T(8,128)(2,1)S(1)}, bf16[96,384]{1,0:T(8,128)(2,1)}, u32[]{:S(2)}) copy-start(bf16[96,384]{1,0:T(8,128)(2,1)} %param.19) | copy-start | bytes 221188
  4.3 9.3 %collective-permute-start.1 = (bf16[96,3,128]{0,2,1:T(8,128)(2,1)S(1)}, bf16[96,3,128]{0,2,1:T(8,128)(2,1)S(1)}, u32[]{:S(2)}, u32[]{:S(2)}) collective-permute-start(bf16[96,3,128]{0,2,1:T(8,128)(2,1)S(1)} %get-tuple-element.90), channel_id=1, source_target_pairs={{4,0},{8,4},{12,8},{16,12},{20,16},{24,20},{28,24},{32,28},{36,32}... | collective-permute-start | bytes 221192 | tf_op jit(solution)/shard_map/ppermute | solution.py:28
  6.9 8.0 %collective-permute-start = (bf16[96,3,128]{0,2,1:T(8,128)(2,1)S(1)}, bf16[96,3,128]{0,2,1:T(8,128)(2,1)S(1)}, u32[]{:S(2)}, u32[]{:S(2)}) collective-permute-start(bf16[96,3,128]{0,2,1:T(8,128)(2,1)S(1)} %get-tuple-element.89), channel_id=1, source_target_pairs={{0,4},{4,8},{8,12},{12,16},{16,20},{20,24},{24,28},{28,32},{32,36}... | collective-permute-start | bytes 221192 | tf_op jit(solution)/shard_map/ppermute | solution.py:25
  13.6 28.6 %copy-start.9 = (bf16[1,96,16,128]{1,3,2,0:T(8,128)(2,1)}, bf16[1,96,16,128]{1,3,2,0:T(8,128)(2,1)S(1)}, u32[]{:S(2)}) copy-start(bf16[1,96,16,128]{1,3,2,0:T(8,128)(2,1)S(1)} %copy.76) | copy-start | bytes 1179652
  77.1 45.1 %copy-start.7 = (f32[96,1,16,8,16]{0,4,3,2,1:T(8,128)S(1)}, f32[96,1,16,8,16]{0,4,3,2,1:T(8,128)}, u32[]{:S(2)}) copy-start(f32[96,1,16,8,16]{0,4,3,2,1:T(8,128)} %copy-done.6) | copy-start | bytes 2359300
  77.1 45.1 %copy-start.12 = (bf16[1,96,16,128]{1,3,2,0:T(8,128)(2,1)S(1)}, bf16[1,96,16,128]{1,3,2,0:T(8,128)(2,1)}, u32[]{:S(2)}) copy-start(bf16[1,96,16,128]{1,3,2,0:T(8,128)(2,1)} %copy-done.11) | copy-start | bytes 1179652
  77.1 45.1 %copy-start.99 = (f32[96]{0:T(128)S(1)}, f32[96]{0:T(128)}, u32[]{:S(2)}) copy-start(f32[96]{0:T(128)} %param.23) | copy-start | bytes 1156
  77.1 6.5 %collective-permute-start.4 = (f32[320,128]{1,0:T(8,128)S(1)}, f32[320,128]{1,0:T(8,128)S(1)}, u32[]{:S(2)}, u32[]{:S(2)}) collective-permute-start(f32[320,128]{1,0:T(8,128)S(1)} %slice_select_fusion), channel_id=1, source_target_pairs={{0,4},{4,0},{8,12},{12,8},{16,20},{20,16},{24,28},{28,24},{32,36},... | collective-permute-start | bytes 491528 | tf_op jit(solution)/shard_map/ppermute | solution.py:35
  83.6 3.7 %collective-permute-start.5 = (f32[160,128]{1,0:T(8,128)S(1)}, f32[160,128]{1,0:T(8,128)S(1)}, u32[]{:S(2)}, u32[]{:S(2)}) collective-permute-start(f32[160,128]{1,0:T(8,128)S(1)} %slice_select_fusion.1), channel_id=1, source_target_pairs={{0,8},{4,12},{8,0},{12,4},{16,24},{20,28},{24,16},{28,20},{32,40},... | collective-permute-start | bytes 245768 | tf_op jit(solution)/shard_map/ppermute | solution.py:35
  87.4 4.3 %collective-permute-start.6 = (f32[80,128]{1,0:T(8,128)S(1)}, f32[80,128]{1,0:T(8,128)S(1)}, u32[]{:S(2)}, u32[]{:S(2)}) collective-permute-start(f32[80,128]{1,0:T(8,128)S(1)} %slice_select_fusion.2), channel_id=1, source_target_pairs={{0,16},{4,20},{8,24},{12,28},{16,0},{20,4},{24,8},{28,12},{32,48},... | collective-permute-start | bytes 122888 | tf_op jit(solution)/shard_map/ppermute | solution.py:35
  91.7 6.6 %collective-permute-start.7 = (f32[40,128]{1,0:T(8,128)S(1)}, f32[40,128]{1,0:T(8,128)S(1)}, u32[]{:S(2)}, u32[]{:S(2)}) collective-permute-start(f32[40,128]{1,0:T(8,128)S(1)} %slice_select_fusion.3), channel_id=1, source_target_pairs={{0,32},{4,36},{8,40},{12,44},{16,48},{20,52},{24,56},{28,60},{32,0... | collective-permute-start | bytes 61448 | tf_op jit(solution)/shard_map/ppermute | solution.py:35
  98.4 2.8 %collective-permute-start.8 = (f32[20,128]{1,0:T(8,128)S(1)}, f32[20,128]{1,0:T(8,128)S(1)}, u32[]{:S(2)}, u32[]{:S(2)}) collective-permute-start(f32[20,128]{1,0:T(8,128)S(1)} %slice_select_fusion.4), channel_id=1, source_target_pairs={{0,64},{4,68},{8,72},{12,76},{16,80},{20,84},{24,88},{28,92},{32,9... | collective-permute-start | bytes 30728 | tf_op jit(solution)/shard_map/ppermute | solution.py:35
  101.2 4.1 %collective-permute-start.9 = (f32[10,128]{1,0:T(8,128)S(1)}, f32[10,128]{1,0:T(8,128)S(1)}, u32[]{:S(2)}, u32[]{:S(2)}) collective-permute-start(f32[10,128]{1,0:T(8,128)S(1)} %slice_select_fusion.5), channel_id=1, source_target_pairs={{0,128},{4,132},{8,136},{12,140},{16,144},{20,148},{24,152},{28,15... | collective-permute-start | bytes 15368 | tf_op jit(solution)/shard_map/ppermute | solution.py:35
  105.3 2.5 %collective-permute-start.10 = (f32[5,128]{1,0:T(8,128)S(1)}, f32[5,128]{1,0:T(8,128)S(1)}, u32[]{:S(2)}, u32[]{:S(2)}) collective-permute-start(f32[5,128]{1,0:T(8,128)S(1)} %slice_select_fusion.6), channel_id=1, source_target_pairs={{0,1},{1,0},{2,3},{3,2},{4,5},{5,4},{6,7},{7,6},{8,9},{9,8},{10,11... | collective-permute-start | bytes 7688 | tf_op jit(solution)/shard_map/ppermute | solution.py:35
  107.8 4.0 %collective-permute-start.11 = (f32[5,128]{1,0:T(8,128)S(1)}, f32[5,128]{1,0:T(8,128)S(1)}, u32[]{:S(2)}, u32[]{:S(2)}) collective-permute-start(f32[5,128]{1,0:T(8,128)S(1)} %select_add_fusion.6), channel_id=1, source_target_pairs={{0,2},{1,3},{2,0},{3,1},{4,6},{5,7},{6,4},{7,5},{8,10},{9,11},{10,... | collective-permute-start | bytes 7688 | tf_op jit(solution)/shard_map/ppermute | solution.py:35
  111.8 2.5 %collective-permute-start.12 = (f32[5,128]{1,0:T(8,128)S(1)}, f32[5,128]{1,0:T(8,128)S(1)}, u32[]{:S(2)}, u32[]{:S(2)}) collective-permute-start(f32[5,128]{1,0:T(8,128)S(1)} %add.562), channel_id=1, source_target_pairs={{0,1},{1,0},{2,3},{3,2},{4,5},{5,4},{6,7},{7,6},{8,9},{9,8},{10,11... | collective-permute-start | bytes 7688 | tf_op jit(solution)/shard_map/ppermute | solution.py:35
  114.3 4.4 %collective-permute-start.13 = (f32[10,128]{1,0:T(8,128)S(1)}, f32[10,128]{1,0:T(8,128)S(1)}, u32[]{:S(2)}, u32[]{:S(2)}) collective-permute-start(f32[10,128]{1,0:T(8,128)S(1)} %maximum_select_fusion.6), channel_id=1, source_target_pairs={{0,128},{4,132},{8,136},{12,140},{16,144},{20,148},{24,152},{28,15... | collective-permute-start | bytes 15368 | tf_op jit(solution)/shard_map/ppermute | solution.py:35
  118.7 2.6 %collective-permute-start.14 = (f32[20,128]{1,0:T(8,128)S(1)}, f32[20,128]{1,0:T(8,128)S(1)}, u32[]{:S(2)}, u32[]{:S(2)}) collective-permute-start(f32[20,128]{1,0:T(8,128)S(1)} %maximum_select_fusion.5), channel_id=1, source_target_pairs={{0,64},{4,68},{8,72},{12,76},{16,80},{20,84},{24,88},{28,92},{32,9... | collective-permute-start | bytes 30728 | tf_op jit(solution)/shard_map/ppermute | solution.py:35
  121.3 6.8 %collective-permute-start.15 = (f32[40,128]{1,0:T(8,128)S(1)}, f32[40,128]{1,0:T(8,128)S(1)}, u32[]{:S(2)}, u32[]{:S(2)}) collective-permute-start(f32[40,128]{1,0:T(8,128)S(1)} %maximum_select_fusion.4), channel_id=1, source_target_pairs={{0,32},{4,36},{8,40},{12,44},{16,48},{20,52},{24,56},{28,60},{32,0... | collective-permute-start | bytes 61448 | tf_op jit(solution)/shard_map/ppermute | solution.py:35
  128.2 23.9 %copy-start.10 = (bf16[1,96,16,128]{1,3,2,0:T(8,128)(2,1)S(1)}, bf16[1,96,16,128]{1,3,2,0:T(8,128)(2,1)}, u32[]{:S(2)}) copy-start(bf16[1,96,16,128]{1,3,2,0:T(8,128)(2,1)} %copy-done.9) | copy-start | bytes 1179652
  128.2 23.9 %copy-start.24 = (f32[96]{0:T(128)S(1)}, f32[96]{0:T(128)}, u32[]{:S(2)}) copy-start(f32[96]{0:T(128)} %copy-done.23) | copy-start | bytes 1156
  128.2 23.9 %copy-start.26 = (f32[96]{0:T(128)S(1)}, f32[96]{0:T(128)}, u32[]{:S(2)}) copy-start(f32[96]{0:T(128)} %copy-done.25) | copy-start | bytes 1156
  128.2 23.9 %copy-start.28 = (f32[96]{0:T(128)S(1)}, f32[96]{0:T(128)}, u32[]{:S(2)}) copy-start(f32[96]{0:T(128)} %copy-done.27) | copy-start | bytes 1156
  128.2 23.9 %copy-start.30 = (f32[96]{0:T(128)S(1)}, f32[96]{0:T(128)}, u32[]{:S(2)}) copy-start(f32[96]{0:T(128)} %copy-done.29) | copy-start | bytes 1156
  128.2 23.9 %copy-start.32 = (f32[96]{0:T(128)S(1)}, f32[96]{0:T(128)}, u32[]{:S(2)}) copy-start(f32[96]{0:T(128)} %copy-done.31) | copy-start | bytes 1156
  128.2 23.9 %copy-start.34 = (f32[96]{0:T(128)S(1)}, f32[96]{0:T(128)}, u32[]{:S(2)}) copy-start(f32[96]{0:T(128)} %copy-done.33) | copy-start | bytes 1156
  128.2 23.9 %copy-start.36 = (f32[96]{0:T(128)S(1)}, f32[96]{0:T(128)}, u32[]{:S(2)}) copy-start(f32[96]{0:T(128)} %copy-done.35) | copy-start | bytes 1156
  128.2 23.9 %copy-start.38 = (f32[96]{0:T(128)S(1)}, f32[96]{0:T(128)}, u32[]{:S(2)}) copy-start(f32[96]{0:T(128)} %copy-done.37) | copy-start | bytes 1156
  128.3 23.9 %copy-start.40 = (f32[96]{0:T(128)S(1)}, f32[96]{0:T(128)}, u32[]{:S(2)}) copy-start(f32[96]{0:T(128)} %copy-done.39) | copy-start | bytes 1156
  128.3 23.9 %copy-start.42 = (f32[96]{0:T(128)S(1)}, f32[96]{0:T(128)}, u32[]{:S(2)}) copy-start(f32[96]{0:T(128)} %copy-done.41) | copy-start | bytes 1156
  128.3 23.9 %copy-start.44 = (f32[96]{0:T(128)S(1)}, f32[96]{0:T(128)}, u32[]{:S(2)}) copy-start(f32[96]{0:T(128)} %copy-done.43) | copy-start | bytes 1156
  128.3 23.9 %copy-start.46 = (f32[96]{0:T(128)S(1)}, f32[96]{0:T(128)}, u32[]{:S(2)}) copy-start(f32[96]{0:T(128)} %copy-done.45) | copy-start | bytes 1156
  128.3 23.9 %copy-start.48 = (f32[96]{0:T(128)S(1)}, f32[96]{0:T(128)}, u32[]{:S(2)}) copy-start(f32[96]{0:T(128)} %copy-done.47) | copy-start | bytes 1156
  128.3 23.9 %copy-start.50 = (f32[96]{0:T(128)S(1)}, f32[96]{0:T(128)}, u32[]{:S(2)}) copy-start(f32[96]{0:T(128)} %copy-done.49) | copy-start | bytes 1156
  128.3 23.9 %copy-start.52 = (f32[96]{0:T(128)S(1)}, f32[96]{0:T(128)}, u32[]{:S(2)}) copy-start(f32[96]{0:T(128)} %copy-done.51) | copy-start | bytes 1156
  128.3 23.9 %copy-start.54 = (f32[96]{0:T(128)S(1)}, f32[96]{0:T(128)}, u32[]{:S(2)}) copy-start(f32[96]{0:T(128)} %copy-done.53) | copy-start | bytes 1156
  128.3 23.9 %copy-start.56 = (f32[96]{0:T(128)S(1)}, f32[96]{0:T(128)}, u32[]{:S(2)}) copy-start(f32[96]{0:T(128)} %copy-done.55) | copy-start | bytes 1156
  128.3 23.9 %copy-start.58 = (f32[96]{0:T(128)S(1)}, f32[96]{0:T(128)}, u32[]{:S(2)}) copy-start(f32[96]{0:T(128)} %copy-done.57) | copy-start | bytes 1156
  128.4 23.9 %copy-start.60 = (f32[96]{0:T(128)S(1)}, f32[96]{0:T(128)}, u32[]{:S(2)}) copy-start(f32[96]{0:T(128)} %copy-done.59) | copy-start | bytes 1156
  128.4 23.9 %copy-start.62 = (f32[96]{0:T(128)S(1)}, f32[96]{0:T(128)}, u32[]{:S(2)}) copy-start(f32[96]{0:T(128)} %copy-done.61) | copy-start | bytes 1156
  128.4 23.9 %copy-start.64 = (f32[96]{0:T(128)S(1)}, f32[96]{0:T(128)}, u32[]{:S(2)}) copy-start(f32[96]{0:T(128)} %copy-done.63) | copy-start | bytes 1156
  128.4 23.9 %copy-start.66 = (f32[96]{0:T(128)S(1)}, f32[96]{0:T(128)}, u32[]{:S(2)}) copy-start(f32[96]{0:T(128)} %copy-done.65) | copy-start | bytes 1156
  128.4 23.9 %copy-start.68 = (f32[96]{0:T(128)S(1)}, f32[96]{0:T(128)}, u32[]{:S(2)}) copy-start(f32[96]{0:T(128)} %copy-done.67) | copy-start | bytes 1156
  128.5 17.0 %collective-permute-start.16 = (f32[80,128]{1,0:T(8,128)S(1)}, f32[80,128]{1,0:T(8,128)S(1)}, u32[]{:S(2)}, u32[]{:S(2)}) collective-permute-start(f32[80,128]{1,0:T(8,128)S(1)} %maximum_select_fusion.3), channel_id=1, source_target_pairs={{0,16},{4,20},{8,24},{12,28},{16,0},{20,4},{24,8},{28,12},{32,48},... | collective-permute-start | bytes 122888 | tf_op jit(solution)/shard_map/ppermute | solution.py:35
  129.8 18.7 %collective-permute-start.3 = (bf16[96,3,128]{0,2,1:T(8,128)(2,1)S(1)}, bf16[96,3,128]{0,2,1:T(8,128)(2,1)S(1)}, u32[]{:S(2)}, u32[]{:S(2)}) collective-permute-start(bf16[96,3,128]{0,2,1:T(8,128)(2,1)S(1)} %get-tuple-element.88), channel_id=1, source_target_pairs={{4,0},{8,4},{12,8},{16,12},{20,16},{24,20},{28,24},{32,28},{36,32}... | collective-permute-start | bytes 221192 | tf_op jit(solution)/shard_map/ppermute | solution.py:28
  143.6 4.8 %collective-permute-start.2 = (bf16[96,3,128]{0,2,1:T(8,128)(2,1)S(1)}, bf16[96,3,128]{0,2,1:T(8,128)(2,1)S(1)}, u32[]{:S(2)}, u32[]{:S(2)}) collective-permute-start(bf16[96,3,128]{0,2,1:T(8,128)(2,1)S(1)} %get-tuple-element.87), channel_id=1, source_target_pairs={{0,4},{4,8},{8,12},{12,16},{16,20},{20,24},{24,28},{28,32},{32,36}... | collective-permute-start | bytes 221192 | tf_op jit(solution)/shard_map/ppermute | solution.py:25
  145.6 5.5 %collective-permute-start.17 = (f32[160,128]{1,0:T(8,128)S(1)}, f32[160,128]{1,0:T(8,128)S(1)}, u32[]{:S(2)}, u32[]{:S(2)}) collective-permute-start(f32[160,128]{1,0:T(8,128)S(1)} %maximum_select_fusion.2), channel_id=1, source_target_pairs={{0,8},{4,12},{8,0},{12,4},{16,24},{20,28},{24,16},{28,20},{32,40},... | collective-permute-start | bytes 245768 | tf_op jit(solution)/shard_map/ppermute | solution.py:35
  151.1 12.8 %collective-permute-start.18 = (f32[320,128]{1,0:T(8,128)S(1)}, f32[320,128]{1,0:T(8,128)S(1)}, u32[]{:S(2)}, u32[]{:S(2)}) collective-permute-start(f32[320,128]{1,0:T(8,128)S(1)} %maximum_select_fusion.1), channel_id=1, source_target_pairs={{0,4},{4,0},{8,12},{12,8},{16,20},{20,16},{24,28},{28,24},{32,36},... | collective-permute-start | bytes 491528 | tf_op jit(solution)/shard_map/ppermute | solution.py:35
  (78 other events, 1012.9 us)

commit v2 on v1

--- a/solution.py
+++ b/solution.py
@@ -118,22 +118,20 @@
     return shaped.reshape(channels, TCOL_DEV * TP, TROWS * TP)
 
 
-def mlp_slots(w_in, w_out, b_in, b_out, x_slots, d_slots):
+def mlp_pixels(w_in, w_out, b_in, b_out, x_pix, d_pix):
     flt = jnp.float32
-    pre_act = (
-        jnp.einsum("cf,scp->sfp", w_in, x_slots, preferred_element_type=flt) + b_in[None, :, None]
-    )
+    pre_act = jnp.einsum("cf,cp->fp", w_in, x_pix, preferred_element_type=flt) + b_in[:, None]
     hidden = rounded(gelu_value(pre_act))
     mlp_out = rounded(
-        jnp.einsum("cf,sfp->scp", w_out, hidden, preferred_element_type=flt) + b_out[None, :, None]
-    )
-    back_hid = jnp.einsum("cf,scp->sfp", w_out, d_slots, preferred_element_type=flt)
+        jnp.einsum("cf,fp->cp", w_out, hidden, preferred_element_type=flt) + b_out[:, None]
+    )
+    back_hid = jnp.einsum("cf,cp->fp", w_out, d_pix, preferred_element_type=flt)
     grad_act = rounded(back_hid * gelu_slope(pre_act))
-    grad_ln = rounded(jnp.einsum("cf,sfp->scp", w_in, grad_act, preferred_element_type=flt))
-    gw_in = jnp.einsum("scp,sfp->cf", x_slots, grad_act, preferred_element_type=flt)
-    gw_out = jnp.einsum("scp,sfp->cf", d_slots, hidden, preferred_element_type=flt)
-    gb_in = jnp.sum(grad_act.astype(flt), axis=(0, 2))
-    gb_out = jnp.sum(d_slots.astype(flt), axis=(0, 2))
+    grad_ln = rounded(jnp.einsum("cf,fp->cp", w_in, grad_act, preferred_element_type=flt))
+    gw_in = jnp.einsum("cp,fp->cf", x_pix, grad_act, preferred_element_type=flt)
+    gw_out = jnp.einsum("cp,fp->cf", d_pix, hidden, preferred_element_type=flt)
+    gb_in = jnp.sum(grad_act.astype(flt), axis=1)
+    gb_out = jnp.sum(d_pix.astype(flt), axis=1)
     return (mlp_out, grad_ln, gw_in, gw_out, gb_in, gb_out)
 
 
@@ -170,18 +168,12 @@
     ln_out = rounded(normed * ln_gain[:, None, None] + ln_bias[:, None, None])
     cot_f = cotangent[0].astype(flt)
     grad_mix = rounded(cot_f * pix_f * layer_scale[:, None, None])
-    flat_live = live_tiles.reshape(-1)
-    tile_count = flat_live.shape[0]
-    tile_order = jnp.argsort((1 - flat_live) * tile_count + jnp.arange(tile_count, dtype=jnp.int32))
-    own_x = to_tiles(ln_out)[tile_order]
-    own_d = to_tiles(grad_mix)[tile_order]
-    mo_slots, dxh_slots, gw_in, gw_out, gb_in, gb_out = mlp_slots(
-        w_in, w_out, b_in, b_out, own_x, own_d
-    )
-    tile_rank = jnp.clip(jnp.cumsum(flat_live) - 1, 0, MOST - 1)
-    keep_tile = flat_live.astype(jnp.bfloat16)[:, None, None]
-    mlp_out = from_tiles(mo_slots[tile_rank] * keep_tile)
-    grad_ln = from_tiles(dxh_slots[tile_rank] * keep_tile)
+    channels, pixels = ln_out.shape[0], strip_w * strip_h
+    mo_flat, dxh_flat, gw_in, gw_out, gb_in, gb_out = mlp_pixels(
+        w_in, w_out, b_in, b_out, ln_out.reshape(channels, pixels), grad_mix.reshape(channels, pixels)
+    )
+    mlp_out = mo_flat.reshape(ln_out.shape) * pixel_mask[None]
+    grad_ln = dxh_flat.reshape(ln_out.shape) * pixel_mask[None]
     out_image = (
         pix_f * (masked.astype(flt) + layer_scale[:, None, None] * mlp_out.astype(flt))
     ).astype(jnp.bfloat16)

time: 168 us -> 147 us (0.88)
  local copies, waits for them, and re-layouts: 30.1 us -> 8.49 us
  starting transfers between devices: 43.2 us -> 52.1 us
  waiting for transfers between devices: 35.7 us -> 27.6 us
  other arithmetic: 45.1 us -> 52.4 us
  matrix products: 10.3 us -> 4.65 us
    ppermute x2, starting transfers between devices: 16.4 us -> 4.1 us  [extended(): lax.ppermute(lax.slice_in_dim(block, 0, width, axis=dim), axis, backward)]
    gather x6 -> x0, local copies, waits for them, and re-layouts: 12.1 us -> none  [the longest x2 4.33 us: on_device(): mlp_out = from_tiles(mo_slots[tile_rank] * keep_tile)]
    ppermute x2, starting transfers between devices: 5.36 us -> 16.8 us  [extended(): lax.ppermute(lax.slice_in_dim(block, block.shape[dim] - width, None, axis...]
    reduce_sum x4, other arithmetic: 9.09 us -> 19.6 us  [kernel_sums(): entries.append(jnp.sum(grad_f * piece, axis=(1, 2)))]
    ppermute x15, starting transfers between devices: 21.4 us -> 31.2 us  [exchanged(): return lax.ppermute(values, axis, [(i, i ^ stride) for i in range(count)])]
    unnamed x219 -> x23, local copies, waits for them, and re-layouts: 8.43 us -> 0.91 us
    ppermute x15, waiting for transfers between devices: 34.5 us -> 27.5 us  [exchanged(): return lax.ppermute(values, axis, [(i, i ^ stride) for i in range(count)])]
    dot_general x6, matrix products: 10.3 us -> 4.65 us  [the longest x1 1.64 us: mlp_pixels(): back_hid = jnp.einsum('cf,cp->fp', w_out, d_pix, preferred_element_type=flt)]
  transfers between devices with their start and end apart: 19 -> 19, of which waited for: 14 -> 13; matrix products, arithmetic and copies ran while one was open for 10% -> 13% of each run, Pallas kernels for 0% -> 0%
where the time goes in v2:
time: 147 us; the launch traced here: 146 us
  other arithmetic  52.4 us (36%)
  starting transfers between devices  52.1 us (35%)
  waiting for transfers between devices  27.6 us (19%)
  local copies, waits for them, and re-layouts  8.49 us (6%)
  matrix products  4.65 us (3%)
    ppermute x15, starting transfers between devices, exchanged(): return lax.ppermute(values, axis, [(i, i ^ stride) for i in range(count)])  31.2 us
    ppermute x15, waiting for transfers between devices, exchanged(): return lax.ppermute(values, axis, [(i, i ^ stride) for i in range(count)])  27.5 us
    reduce_sum x4, other arithmetic, kernel_sums(): entries.append(jnp.sum(grad_f * piece, axis=(1, 2)))  19.6 us
    ppermute x2, starting transfers between devices, extended(): lax.ppermute(lax.slice_in_dim(block, block.shape[dim] - width, None, axis...  16.8 us
    broadcast_in_dim x1, other arithmetic, on_device(): grad_image[None]  11.8 us
    reduce_sum x1, other arithmetic, on_device(): centered = pre - jnp.mean(pre, axis=0, keepdims=True)  11.5 us
    ppermute x2, starting transfers between devices, extended(): lax.ppermute(lax.slice_in_dim(block, 0, width, axis=dim), axis, backward)  4.1 us
  transfers between devices with their start and end apart: 19, of which 13 were waited for; matrix products, arithmetic and copies ran while one was open for 13% of the time, Pallas kernels for 0%

profile of v2, /device:TPU:3, one launch (start us, length us, event | category | flops | bytes accessed | tf_op | source)
XLA Modules:
  0.0 146.4 jit_solution(15302407349582157760)
XLA Ops:
  0.7 0.7 convert_bitcast_fusion
  1.5 1.0 bitcast_multiply_fusion.5
  2.6 4.1 %collective-permute-start = (bf16[96,3,128]{2,1,0:T(4,128)(2,1)S(1)}, bf16[96,3,128]{2,1,0:T(4,128)(2,1)S(1)}, u32[]{:S(2)}, u32[]{:S(2)}) collective-permute-start(bf16[96,3,128]{2,1,0:T(4,128)(2,1)S(1)} %get-tuple-element.74), channel_id=1, source_target_pairs={{0,4},{4,8},{8,12},{12,16},{16,20},{20,24},{24,28},{28,32},{32,36}... | collective-permute-start | bytes 221192 | tf_op jit(solution)/shard_map/ppermute | solution.py:25
  6.8 1.9 %collective-permute-start.1 = (bf16[96,3,128]{2,1,0:T(4,128)(2,1)S(1)}, bf16[96,3,128]{2,1,0:T(4,128)(2,1)S(1)}, u32[]{:S(2)}, u32[]{:S(2)}) collective-permute-start(bf16[96,3,128]{2,1,0:T(4,128)(2,1)S(1)} %get-tuple-element.75), channel_id=1, source_target_pairs={{4,0},{8,4},{12,8},{16,12},{20,16},{24,20},{28,24},{32,28},{36,32}... | collective-permute-start | bytes 221192 | tf_op jit(solution)/shard_map/ppermute | solution.py:28
  8.7 1.0 slice_bitcast_fusion.47
  9.7 1.0 slice_bitcast_fusion.48
  10.7 0.9 slice_bitcast_fusion.46
  11.7 1.2 fusion.19
  12.8 0.8 convert_reduce_fusion.3
  13.6 1.0 select_maximum_fusion.2
  14.7 11.5 %fusion.170 = (f32[16,128]{1,0:T(8,128)S(1)}, f32[96,16,128]{2,1,0:T(8,128)S(1)}) fusion(f32[96]{0:T(128)S(1)} %copy-done.7, bf16[96,22,134]{2,1,0:T(8,128)(2,1)S(1)} %select_maximum_fusion.2, f32[96]{0:T(128)S(1)} %get-tuple-element.123, f32[96]{0:T(128)S(1)} %get-tuple-element.124, f32[96]{0:T(128)S(1)} %get-tuple-element.77, ...), kind=kLoop, calls=%fused_computation.401 | loop fusion | flops 32634880 | bytes 17869568 | tf_op jit(solution)/shard_map/reduce_sum | solution.py:165
  26.8 1.0 fusion.7
  27.7 1.6 %fusion.5 = bf16[384,2048]{0,1:T(8,128)(2,1)S(1)} fusion(f32[2048,384]{1,0:T(8,128)S(1)} %get-tuple-element.126, bf16[96,384]{1,0:T(8,128)(2,1)S(1)} %copy-done.3, bf16[12,8,16,128]{3,2,1,0:T(8,128)(2,1)S(1)} %bitcast.245), kind=kOutput, calls=%fused_computation.59 | convolution fusion | flops 158859264 | bytes 5185536 | tf_op jit(solution)/shard_map/cf,cp->fp/dot_general | solution.py:128
  30.8 1.2 fusion.73
  32.5 7.6 %fusion.149 = (f32[96]{0:T(128)S(1)}, f32[96]{0:T(128)S(1)}, f32[96]{0:T(128)S(1)}, f32[96]{0:T(128)S(1)}, f32[96]{0:T(128)S(1)}, /*index=5*/f32[96]{0:T(128)S(1...) fusion(bf16[96,16,128]{2,1,0:T(8,128)(2,1)S(1)} %fusion.23, ...), kind=kLoop, calls=%fused_computation.270 | loop fusion | flops 10811712 | bytes 7478016 | tf_op jit(solution)/shard_map/reduce_sum | solution.py:105
  40.1 7.6 %fusion.150 = (f32[96]{0:T(128)S(1)}, f32[96]{0:T(128)S(1)}, f32[96]{0:T(128)S(1)}, f32[96]{0:T(128)S(1)}, f32[96]{0:T(128)S(1)}, /*index=5*/f32[96]{0:T(128)S(1...) fusion(bf16[96,16,128]{2,1,0:T(8,128)(2,1)S(1)} %fusion.23, ...), kind=kLoop, calls=%fused_computation.271 | loop fusion | flops 10811712 | bytes 7478016 | tf_op jit(solution)/shard_map/reduce_sum | solution.py:105
  47.7 2.1 %fusion.148 = (f32[96]{0:T(128)S(1)}, f32[96]{0:T(128)S(1)}, f32[96]{0:T(128)S(1)}, f32[96]{0:T(128)S(1)}, f32[96]{0:T(128)S(1)}, /*index=5*/f32[96]{0:T(128)S(1)}) fusion(bf16[96,16,128]{2,1,0:T(8,128)(2,1)S(1)} %fusion.23, bf16[96,22,134]{2,1,0:T(8,128)(2,1)S(1)} %select_maximum_fusion.2), kind=kLoop, calls=%fused_computation.269 | loop fusion | flops 3734976 | bytes 2754816 | tf_op jit(solution)/shard_map/reduce_sum | solution.py:105
  51.1 2.3 %fusion.147 = (f32[96]{0:T(128)S(1)}, f32[96]{0:T(128)S(1)}, f32[96]{0:T(128)S(1)}, f32[96]{0:T(128)S(1)}, f32[96]{0:T(128)S(1)}, /*index=5*/f32[96]{0:T(128)S(1)}, f32[96]{0:T(128)S(1)}, f32[96]{0:T(128)S(1)}) fusion(bf16[96,16,128]{2,1,0:T(8,128)(2,1)S(1)} %fusion.23, bf16[96,3,128]{2,1,0:T(4,128)(2,1)S(1)} %collective-permute-done.1, ...), kind=kLoop, calls=%fused_computation.268 | loop fusion | flops 8060160 | bytes 936960 | tf_op jit(solution)/shard_map/reduce_sum | solution.py:105
  54.0 1.4 concatenate.77
  55.4 3.8 %collective-permute-start.4 = (f32[320,128]{1,0:T(8,128)S(1)}, f32[320,128]{1,0:T(8,128)S(1)}, u32[]{:S(2)}, u32[]{:S(2)}) collective-permute-start(f32[320,128]{1,0:T(8,128)S(1)} %slice_select_fusion), channel_id=1, source_target_pairs={{0,4},{4,0},{8,12},{12,8},{16,20},{20,16},{24,28},{28,24},{32,36},... | collective-permute-start | bytes 491528 | tf_op jit(solution)/shard_map/ppermute | solution.py:35
  59.2 1.0 collective-permute-done.4
  60.4 3.6 %collective-permute-done.5 = f32[160,128]{1,0:T(8,128)S(1)} collective-permute-done((f32[160,128]{1,0:T(8,128)S(1)}, f32[160,128]{1,0:T(8,128)S(1)}, u32[]{:S(2)}, u32[]{:S(2)}) %collective-permute-start.5) | collective-permute-done | bytes 81952 | tf_op jit(solution)/shard_map/ppermute | solution.py:35
  64.1 1.8 %collective-permute-start.6 = (f32[80,128]{1,0:T(8,128)S(1)}, f32[80,128]{1,0:T(8,128)S(1)}, u32[]{:S(2)}, u32[]{:S(2)}) collective-permute-start(f32[80,128]{1,0:T(8,128)S(1)} %slice_select_fusion.2), channel_id=1, source_target_pairs={{0,16},{4,20},{8,24},{12,28},{16,0},{20,4},{24,8},{28,12},{32,48},... | collective-permute-start | bytes 122888 | tf_op jit(solution)/shard_map/ppermute | solution.py:35
  65.9 2.4 %collective-permute-done.6 = f32[80,128]{1,0:T(8,128)S(1)} collective-permute-done((f32[80,128]{1,0:T(8,128)S(1)}, f32[80,128]{1,0:T(8,128)S(1)}, u32[]{:S(2)}, u32[]{:S(2)}) %collective-permute-start.6) | collective-permute-done | bytes 40992 | tf_op jit(solution)/shard_map/ppermute | solution.py:35
  68.4 4.7 %collective-permute-start.7 = (f32[40,128]{1,0:T(8,128)S(1)}, f32[40,128]{1,0:T(8,128)S(1)}, u32[]{:S(2)}, u32[]{:S(2)}) collective-permute-start(f32[40,128]{1,0:T(8,128)S(1)} %slice_select_fusion.3), channel_id=1, source_target_pairs={{0,32},{4,36},{8,40},{12,44},{16,48},{20,52},{24,56},{28,60},{32,0... | collective-permute-start | bytes 61448 | tf_op jit(solution)/shard_map/ppermute | solution.py:35
  73.0 1.9 %collective-permute-done.7 = f32[40,128]{1,0:T(8,128)S(1)} collective-permute-done((f32[40,128]{1,0:T(8,128)S(1)}, f32[40,128]{1,0:T(8,128)S(1)}, u32[]{:S(2)}, u32[]{:S(2)}) %collective-permute-start.7) | collective-permute-done | bytes 20512 | tf_op jit(solution)/shard_map/ppermute | solution.py:35
  75.1 2.8 %collective-permute-done.8 = f32[20,128]{1,0:T(8,128)S(1)} collective-permute-done((f32[20,128]{1,0:T(8,128)S(1)}, f32[20,128]{1,0:T(8,128)S(1)}, u32[]{:S(2)}, u32[]{:S(2)}) %collective-permute-start.8) | collective-permute-done | bytes 10272 | tf_op jit(solution)/shard_map/ppermute | solution.py:35
  77.9 2.2 %collective-permute-start.9 = (f32[10,128]{1,0:T(8,128)S(1)}, f32[10,128]{1,0:T(8,128)S(1)}, u32[]{:S(2)}, u32[]{:S(2)}) collective-permute-start(f32[10,128]{1,0:T(8,128)S(1)} %slice_select_fusion.5), channel_id=1, source_target_pairs={{0,128},{4,132},{8,136},{12,140},{16,144},{20,148},{24,152},{28,15... | collective-permute-start | bytes 15368 | tf_op jit(solution)/shard_map/ppermute | solution.py:35
  80.1 1.9 %collective-permute-done.9 = f32[10,128]{1,0:T(8,128)S(1)} collective-permute-done((f32[10,128]{1,0:T(8,128)S(1)}, f32[10,128]{1,0:T(8,128)S(1)}, u32[]{:S(2)}, u32[]{:S(2)}) %collective-permute-start.9) | collective-permute-done | bytes 5152 | tf_op jit(solution)/shard_map/ppermute | solution.py:35
  82.0 1.4 collective-permute-start.10
  83.4 1.2 collective-permute-done.10
  84.6 2.9 %collective-permute-start.11 = (f32[5,128]{1,0:T(8,128)S(1)}, f32[5,128]{1,0:T(8,128)S(1)}, u32[]{:S(2)}, u32[]{:S(2)}) collective-permute-start(f32[5,128]{1,0:T(8,128)S(1)} %select_add_fusion.6), channel_id=1, source_target_pairs={{0,2},{1,3},{2,0},{3,1},{4,6},{5,7},{6,4},{7,5},{8,10},{9,11},{10,... | collective-permute-start | bytes 7688 | tf_op jit(solution)/shard_map/ppermute | solution.py:35
  87.5 1.1 collective-permute-done.11
  88.6 1.3 collective-permute-start.12
  89.9 1.2 collective-permute-done.12
  91.0 2.2 %collective-permute-start.13 = (f32[10,128]{1,0:T(8,128)S(1)}, f32[10,128]{1,0:T(8,128)S(1)}, u32[]{:S(2)}, u32[]{:S(2)}) collective-permute-start(f32[10,128]{1,0:T(8,128)S(1)} %maximum_select_fusion.6), channel_id=1, source_target_pairs={{0,128},{4,132},{8,136},{12,140},{16,144},{20,148},{24,152},{28,15... | collective-permute-start | bytes 15368 | tf_op jit(solution)/shard_map/ppermute | solution.py:35
  93.2 2.2 %collective-permute-done.13 = f32[10,128]{1,0:T(8,128)S(1)} collective-permute-done((f32[10,128]{1,0:T(8,128)S(1)}, f32[10,128]{1,0:T(8,128)S(1)}, u32[]{:S(2)}, u32[]{:S(2)}) %collective-permute-start.13) | collective-permute-done | bytes 5152 | tf_op jit(solution)/shard_map/ppermute | solution.py:35
  95.8 2.5 %collective-permute-done.14 = f32[20,128]{1,0:T(8,128)S(1)} collective-permute-done((f32[20,128]{1,0:T(8,128)S(1)}, f32[20,128]{1,0:T(8,128)S(1)}, u32[]{:S(2)}, u32[]{:S(2)}) %collective-permute-start.14) | collective-permute-done | bytes 10272 | tf_op jit(solution)/shard_map/ppermute | solution.py:35
  98.3 4.6 %collective-permute-start.15 = (f32[40,128]{1,0:T(8,128)S(1)}, f32[40,128]{1,0:T(8,128)S(1)}, u32[]{:S(2)}, u32[]{:S(2)}) collective-permute-start(f32[40,128]{1,0:T(8,128)S(1)} %maximum_select_fusion.4), channel_id=1, source_target_pairs={{0,32},{4,36},{8,40},{12,44},{16,48},{20,52},{24,56},{28,60},{32,0... | collective-permute-start | bytes 61448 | tf_op jit(solution)/shard_map/ppermute | solution.py:35
  103.0 12.7 %collective-permute-start.2 = (bf16[96,3,128]{2,1,0:T(4,128)(2,1)S(1)}, bf16[96,3,128]{2,1,0:T(4,128)(2,1)S(1)}, u32[]{:S(2)}, u32[]{:S(2)}) collective-permute-start(bf16[96,3,128]{2,1,0:T(4,128)(2,1)S(1)} %get-tuple-element.72), channel_id=1, source_target_pairs={{0,4},{4,8},{8,12},{12,16},{16,20},{20,24},{24,28},{28,32},{32,36}... | collective-permute-start | bytes 221192 | tf_op jit(solution)/shard_map/ppermute | solution.py:25
  115.8 2.2 %collective-permute-start.3 = (bf16[96,3,128]{2,1,0:T(4,128)(2,1)S(1)}, bf16[96,3,128]{2,1,0:T(4,128)(2,1)S(1)}, u32[]{:S(2)}, u32[]{:S(2)}) collective-permute-start(bf16[96,3,128]{2,1,0:T(4,128)(2,1)S(1)} %get-tuple-element.73), channel_id=1, source_target_pairs={{4,0},{8,4},{12,8},{16,12},{20,16},{24,20},{28,24},{32,28},{36,32}... | collective-permute-start | bytes 221192 | tf_op jit(solution)/shard_map/ppermute | solution.py:28
  118.5 1.0 multiply_convert_fusion
  119.5 3.0 %collective-permute-done.16 = f32[80,128]{1,0:T(8,128)S(1)} collective-permute-done((f32[80,128]{1,0:T(8,128)S(1)}, f32[80,128]{1,0:T(8,128)S(1)}, u32[]{:S(2)}, u32[]{:S(2)}) %collective-permute-start.16) | collective-permute-done | bytes 40992 | tf_op jit(solution)/shard_map/ppermute | solution.py:35
  122.7 1.0 select_maximum_fusion
  123.7 2.7 %collective-permute-done.17 = f32[160,128]{1,0:T(8,128)S(1)} collective-permute-done((f32[160,128]{1,0:T(8,128)S(1)}, f32[160,128]{1,0:T(8,128)S(1)}, u32[]{:S(2)}, u32[]{:S(2)}) %collective-permute-start.17) | collective-permute-done | bytes 81952 | tf_op jit(solution)/shard_map/ppermute | solution.py:35
  126.4 5.1 %collective-permute-start.18 = (f32[320,128]{1,0:T(8,128)S(1)}, f32[320,128]{1,0:T(8,128)S(1)}, u32[]{:S(2)}, u32[]{:S(2)}) collective-permute-start(f32[320,128]{1,0:T(8,128)S(1)} %maximum_select_fusion.1), channel_id=1, source_target_pairs={{0,4},{4,0},{8,12},{12,8},{16,20},{20,16},{24,28},{28,24},{32,36},... | collective-permute-start | bytes 491528 | tf_op jit(solution)/shard_map/ppermute | solution.py:35
  131.5 11.8 %fusion.164 = bf16[1,96,16,128]{3,2,1,0:T(8,128)(2,1)} fusion(bf16[96,22,134]{2,1,0:T(8,128)(2,1)S(1)} %select_maximum_fusion, f32[96]{0:T(128)S(1)} %get-tuple-element.76, f32[96]{0:T(128)S(1)} %get-tuple-element.95, f32[96]{0:T(128)S(1)} %get-tuple-element.114, bf16[96,3,128]{2,1,0:T(4,128)(2,1)S(1)} %collective-permute-done.3, ...), kind=kLoop, calls=%fused_computation.314 | loop fusion | flops 33030144 | bytes 17861504 | tf_op jit(solution)/shard_map/broadcast_in_dim | solution.py:211
  144.1 0.8 reshape.235
  (92 shorter events, 8.1 us)
Async XLA Ops:
  0.6 26.1 %copy-start = (bf16[96,384]{1,0:T(8,128)(2,1)S(1)}, bf16[96,384]{1,0:T(8,128)(2,1)}, u32[]{:S(2)}) copy-start(bf16[96,384]{1,0:T(8,128)(2,1)} %param.19) | copy-start | bytes 221188
  0.6 14.1 %copy-start.7 = (f32[96]{0:T(128)S(1)}, f32[96]{0:T(128)}, u32[]{:S(2)}) copy-start(f32[96]{0:T(128)} %param.16) | copy-start | bytes 1156
  2.6 11.0 %collective-permute-start = (bf16[96,3,128]{2,1,0:T(4,128)(2,1)S(1)}, bf16[96,3,128]{2,1,0:T(4,128)(2,1)S(1)}, u32[]{:S(2)}, u32[]{:S(2)}) collective-permute-start(bf16[96,3,128]{2,1,0:T(4,128)(2,1)S(1)} %get-tuple-element.74), channel_id=1, source_target_pairs={{0,4},{4,8},{8,12},{12,16},{16,20},{20,24},{24,28},{28,32},{32,36}... | collective-permute-start | bytes 221192 | tf_op jit(solution)/shard_map/ppermute | solution.py:25
  6.8 6.9 %collective-permute-start.1 = (bf16[96,3,128]{2,1,0:T(4,128)(2,1)S(1)}, bf16[96,3,128]{2,1,0:T(4,128)(2,1)S(1)}, u32[]{:S(2)}, u32[]{:S(2)}) collective-permute-start(bf16[96,3,128]{2,1,0:T(4,128)(2,1)S(1)} %get-tuple-element.75), channel_id=1, source_target_pairs={{4,0},{8,4},{12,8},{16,12},{20,16},{24,20},{28,24},{32,28},{36,32}... | collective-permute-start | bytes 221192 | tf_op jit(solution)/shard_map/ppermute | solution.py:28
  14.7 11.7 %copy-start.4 = (f32[96]{0:T(128)S(1)}, f32[96]{0:T(128)}, u32[]{:S(2)}) copy-start(f32[96]{0:T(128)} %param.17) | copy-start | bytes 1156
  14.7 11.7 %copy-start.8 = (f32[96]{0:T(128)S(1)}, f32[96]{0:T(128)}, u32[]{:S(2)}) copy-start(f32[96]{0:T(128)} %param.18) | copy-start | bytes 1156
  14.7 12.0 %copy-start.6 = (f32[384]{0:T(512)S(1)}, f32[384]{0:T(512)}, u32[]{:S(2)}) copy-start(f32[384]{0:T(512)} %param.20) | copy-start | bytes 4612
  26.8 1.0 copy-start.3
  29.4 0.7 copy-start.9
  29.4 1.4 copy-start.1
  53.4 65.1 %copy-start.2 = (bf16[1,96,16,128]{3,2,1,0:T(8,128)(2,1)S(1)}, bf16[1,96,16,128]{3,2,1,0:T(8,128)(2,1)}, u32[]{:S(2)}) copy-start(bf16[1,96,16,128]{3,2,1,0:T(8,128)(2,1)} %param.12) | copy-start | bytes 1179652
  53.4 65.1 %copy-start.5 = (f32[96]{0:T(128)S(1)}, f32[96]{0:T(128)}, u32[]{:S(2)}) copy-start(f32[96]{0:T(128)} %param.23) | copy-start | bytes 1156
  55.4 4.9 %collective-permute-start.4 = (f32[320,128]{1,0:T(8,128)S(1)}, f32[320,128]{1,0:T(8,128)S(1)}, u32[]{:S(2)}, u32[]{:S(2)}) collective-permute-start(f32[320,128]{1,0:T(8,128)S(1)} %slice_select_fusion), channel_id=1, source_target_pairs={{0,4},{4,0},{8,12},{12,8},{16,20},{20,16},{24,28},{28,24},{32,36},... | collective-permute-start | bytes 491528 | tf_op jit(solution)/shard_map/ppermute | solution.py:35
  60.3 3.7 %collective-permute-start.5 = (f32[160,128]{1,0:T(8,128)S(1)}, f32[160,128]{1,0:T(8,128)S(1)}, u32[]{:S(2)}, u32[]{:S(2)}) collective-permute-start(f32[160,128]{1,0:T(8,128)S(1)} %slice_select_fusion.1), channel_id=1, source_target_pairs={{0,8},{4,12},{8,0},{12,4},{16,24},{20,28},{24,16},{28,20},{32,40},... | collective-permute-start | bytes 245768 | tf_op jit(solution)/shard_map/ppermute | solution.py:35
  64.1 4.3 %collective-permute-start.6 = (f32[80,128]{1,0:T(8,128)S(1)}, f32[80,128]{1,0:T(8,128)S(1)}, u32[]{:S(2)}, u32[]{:S(2)}) collective-permute-start(f32[80,128]{1,0:T(8,128)S(1)} %slice_select_fusion.2), channel_id=1, source_target_pairs={{0,16},{4,20},{8,24},{12,28},{16,0},{20,4},{24,8},{28,12},{32,48},... | collective-permute-start | bytes 122888 | tf_op jit(solution)/shard_map/ppermute | solution.py:35
  68.4 6.6 %collective-permute-start.7 = (f32[40,128]{1,0:T(8,128)S(1)}, f32[40,128]{1,0:T(8,128)S(1)}, u32[]{:S(2)}, u32[]{:S(2)}) collective-permute-start(f32[40,128]{1,0:T(8,128)S(1)} %slice_select_fusion.3), channel_id=1, source_target_pairs={{0,32},{4,36},{8,40},{12,44},{16,48},{20,52},{24,56},{28,60},{32,0... | collective-permute-start | bytes 61448 | tf_op jit(solution)/shard_map/ppermute | solution.py:35
  75.0 2.9 %collective-permute-start.8 = (f32[20,128]{1,0:T(8,128)S(1)}, f32[20,128]{1,0:T(8,128)S(1)}, u32[]{:S(2)}, u32[]{:S(2)}) collective-permute-start(f32[20,128]{1,0:T(8,128)S(1)} %slice_select_fusion.4), channel_id=1, source_target_pairs={{0,64},{4,68},{8,72},{12,76},{16,80},{20,84},{24,88},{28,92},{32,9... | collective-permute-start | bytes 30728 | tf_op jit(solution)/shard_map/ppermute | solution.py:35
  77.9 4.1 %collective-permute-start.9 = (f32[10,128]{1,0:T(8,128)S(1)}, f32[10,128]{1,0:T(8,128)S(1)}, u32[]{:S(2)}, u32[]{:S(2)}) collective-permute-start(f32[10,128]{1,0:T(8,128)S(1)} %slice_select_fusion.5), channel_id=1, source_target_pairs={{0,128},{4,132},{8,136},{12,140},{16,144},{20,148},{24,152},{28,15... | collective-permute-start | bytes 15368 | tf_op jit(solution)/shard_map/ppermute | solution.py:35
  82.0 2.5 %collective-permute-start.10 = (f32[5,128]{1,0:T(8,128)S(1)}, f32[5,128]{1,0:T(8,128)S(1)}, u32[]{:S(2)}, u32[]{:S(2)}) collective-permute-start(f32[5,128]{1,0:T(8,128)S(1)} %slice_select_fusion.6), channel_id=1, source_target_pairs={{0,1},{1,0},{2,3},{3,2},{4,5},{5,4},{6,7},{7,6},{8,9},{9,8},{10,11... | collective-permute-start | bytes 7688 | tf_op jit(solution)/shard_map/ppermute | solution.py:35
  84.6 4.0 %collective-permute-start.11 = (f32[5,128]{1,0:T(8,128)S(1)}, f32[5,128]{1,0:T(8,128)S(1)}, u32[]{:S(2)}, u32[]{:S(2)}) collective-permute-start(f32[5,128]{1,0:T(8,128)S(1)} %select_add_fusion.6), channel_id=1, source_target_pairs={{0,2},{1,3},{2,0},{3,1},{4,6},{5,7},{6,4},{7,5},{8,10},{9,11},{10,... | collective-permute-start | bytes 7688 | tf_op jit(solution)/shard_map/ppermute | solution.py:35
  88.6 2.5 %collective-permute-start.12 = (f32[5,128]{1,0:T(8,128)S(1)}, f32[5,128]{1,0:T(8,128)S(1)}, u32[]{:S(2)}, u32[]{:S(2)}) collective-permute-start(f32[5,128]{1,0:T(8,128)S(1)} %add.533), channel_id=1, source_target_pairs={{0,1},{1,0},{2,3},{3,2},{4,5},{5,4},{6,7},{7,6},{8,9},{9,8},{10,11... | collective-permute-start | bytes 7688 | tf_op jit(solution)/shard_map/ppermute | solution.py:35
  91.0 4.4 %collective-permute-start.13 = (f32[10,128]{1,0:T(8,128)S(1)}, f32[10,128]{1,0:T(8,128)S(1)}, u32[]{:S(2)}, u32[]{:S(2)}) collective-permute-start(f32[10,128]{1,0:T(8,128)S(1)} %maximum_select_fusion.6), channel_id=1, source_target_pairs={{0,128},{4,132},{8,136},{12,140},{16,144},{20,148},{24,152},{28,15... | collective-permute-start | bytes 15368 | tf_op jit(solution)/shard_map/ppermute | solution.py:35
  95.4 2.9 %collective-permute-start.14 = (f32[20,128]{1,0:T(8,128)S(1)}, f32[20,128]{1,0:T(8,128)S(1)}, u32[]{:S(2)}, u32[]{:S(2)}) collective-permute-start(f32[20,128]{1,0:T(8,128)S(1)} %maximum_select_fusion.5), channel_id=1, source_target_pairs={{0,64},{4,68},{8,72},{12,76},{16,80},{20,84},{24,88},{28,92},{32,9... | collective-permute-start | bytes 30728 | tf_op jit(solution)/shard_map/ppermute | solution.py:35
  98.3 19.6 %collective-permute-start.15 = (f32[40,128]{1,0:T(8,128)S(1)}, f32[40,128]{1,0:T(8,128)S(1)}, u32[]{:S(2)}, u32[]{:S(2)}) collective-permute-start(f32[40,128]{1,0:T(8,128)S(1)} %maximum_select_fusion.4), channel_id=1, source_target_pairs={{0,32},{4,36},{8,40},{12,44},{16,48},{20,52},{24,56},{28,60},{32,0... | collective-permute-start | bytes 61448 | tf_op jit(solution)/shard_map/ppermute | solution.py:35
  103.0 19.6 %collective-permute-start.2 = (bf16[96,3,128]{2,1,0:T(4,128)(2,1)S(1)}, bf16[96,3,128]{2,1,0:T(4,128)(2,1)S(1)}, u32[]{:S(2)}, u32[]{:S(2)}) collective-permute-start(bf16[96,3,128]{2,1,0:T(4,128)(2,1)S(1)} %get-tuple-element.72), channel_id=1, source_target_pairs={{0,4},{4,8},{8,12},{12,16},{16,20},{20,24},{24,28},{28,32},{32,36}... | collective-permute-start | bytes 221192 | tf_op jit(solution)/shard_map/ppermute | solution.py:25
  115.8 6.9 %collective-permute-start.3 = (bf16[96,3,128]{2,1,0:T(4,128)(2,1)S(1)}, bf16[96,3,128]{2,1,0:T(4,128)(2,1)S(1)}, u32[]{:S(2)}, u32[]{:S(2)}) collective-permute-start(bf16[96,3,128]{2,1,0:T(4,128)(2,1)S(1)} %get-tuple-element.73), channel_id=1, source_target_pairs={{4,0},{8,4},{12,8},{16,12},{20,16},{24,20},{28,24},{32,28},{36,32}... | collective-permute-start | bytes 221192 | tf_op jit(solution)/shard_map/ppermute | solution.py:28
  118.0 4.6 %collective-permute-start.16 = (f32[80,128]{1,0:T(8,128)S(1)}, f32[80,128]{1,0:T(8,128)S(1)}, u32[]{:S(2)}, u32[]{:S(2)}) collective-permute-start(f32[80,128]{1,0:T(8,128)S(1)} %maximum_select_fusion.3), channel_id=1, source_target_pairs={{0,16},{4,20},{8,24},{12,28},{16,0},{20,4},{24,8},{28,12},{32,48},... | collective-permute-start | bytes 122888 | tf_op jit(solution)/shard_map/ppermute | solution.py:35
  122.5 3.9 %collective-permute-start.17 = (f32[160,128]{1,0:T(8,128)S(1)}, f32[160,128]{1,0:T(8,128)S(1)}, u32[]{:S(2)}, u32[]{:S(2)}) collective-permute-start(f32[160,128]{1,0:T(8,128)S(1)} %maximum_select_fusion.2), channel_id=1, source_target_pairs={{0,8},{4,12},{8,0},{12,4},{16,24},{20,28},{24,16},{28,20},{32,40},... | collective-permute-start | bytes 245768 | tf_op jit(solution)/shard_map/ppermute | solution.py:35
  126.4 16.9 %collective-permute-start.18 = (f32[320,128]{1,0:T(8,128)S(1)}, f32[320,128]{1,0:T(8,128)S(1)}, u32[]{:S(2)}, u32[]{:S(2)}) collective-permute-start(f32[320,128]{1,0:T(8,128)S(1)} %maximum_select_fusion.1), channel_id=1, source_target_pairs={{0,4},{4,0},{8,12},{12,8},{16,20},{20,16},{24,28},{28,24},{32,36},... | collective-permute-start | bytes 491528 | tf_op jit(solution)/shard_map/ppermute | solution.py:35
